TPU v7x, 32 devices: a whole 2x2x4 slice. The times are simulated.
32 devices in a mesh: gz: 8 (over z, core), grp: 4 (over y, x).
Axes of the slice: x: 2, y: 2, z: 4, core: 2. Of those that a mesh axis runs over, the one named last changes fastest.
Arguments:
- volumes: bfloat16 [4, 16, 16, 1024], P('grp', 'gz'), may hold values from -6 to 6
- cotangent: bfloat16 [4, 8, 64, 128], P(None, 'gz', None, 'grp'), may hold values from -6 to 6
- fine_kernel: bfloat16 [1728, 64], replicated, may hold values from -0.15625 to 0.15625
- down_kernel: bfloat16 [512, 128], replicated, may hold values from -0.25 to 0.25
- coarse_kernel: bfloat16 [3456, 128], P(None, 'grp'), may hold values from -0.109375 to 0.109375
Outputs:
- coarse_out: bfloat16 [4, 8, 64, 128], P(None, 'gz', None, 'grp')
- volume_grad: bfloat16 [4, 16, 16, 1024], P('grp', 'gz')
- fine_kernel_grad: float32 [1728, 64], replicated
- down_kernel_grad: float32 [512, 128], replicated
- coarse_kernel_grad: float32 [3456, 128], P(None, 'grp')
All inputs are finite; a program needn't handle non-finite values.
Results may differ from a plain program's by a relative error of at most 0.019.
Values may be sent and summed in bfloat16 or wider, within the bound.
A program may use at most 64 MiB of HBM per device.

v0:
```python
import jax
import jax.numpy as jnp
from jax import lax
from jax.sharding import PartitionSpec as P


def with_halo(array, sides, width):
    for axis, dim in sides:
        devices, length = (lax.axis_size(axis), array.shape[dim])
        up = [(i, (i + 1) % devices) for i in range(devices - 1)]
        down = [(j, i) for i, j in up]
        last = lax.slice_in_dim(array, length - width, length, axis=dim)
        initial = lax.slice_in_dim(array, 0, width, axis=dim)
        before = lax.ppermute(last, axis, up)
        after = lax.ppermute(initial, axis, down)
        array = jnp.concatenate([before, array, after], axis=dim)
    return array


def pad_sides(block):
    return jnp.pad(block, ((0, 0), (0, 0), (1, 1), (1, 1), (0, 0)))


def convolve(padded, kernel):
    samples, extent_z, extent_x, extent_y, channels = padded.shape
    extent_z, extent_x, extent_y = (extent_z - 2, extent_x - 2, extent_y - 2)
    summed = None
    for plane in range(3):
        pieces = [
            padded[
                :,
                plane : plane + extent_z,
                row_step : row_step + extent_x,
                col_step : col_step + extent_y,
                :,
            ]
            for row_step in range(3)
            for col_step in range(3)
        ]
        columns = jnp.concatenate(pieces, axis=-1).reshape(-1, 9 * channels)
        rows = kernel[plane * 9 * channels : (plane + 1) * 9 * channels]
        partial_value = jnp.dot(columns, rows, preferred_element_type=jnp.float32)
        summed = partial_value if summed is None else summed + partial_value
    return summed.reshape(samples, extent_z, extent_x, extent_y, -1)


def kernel_gradient(padded, grad):
    samples, extent_z, extent_x, extent_y, channels = padded.shape
    extent_z, extent_x, extent_y = (extent_z - 2, extent_x - 2, extent_y - 2)
    flat_grad = grad.reshape(-1, grad.shape[-1])
    blocks = []
    for plane in range(3):
        pieces = [
            padded[
                :,
                plane : plane + extent_z,
                row_step : row_step + extent_x,
                col_step : col_step + extent_y,
                :,
            ]
            for row_step in range(3)
            for col_step in range(3)
        ]
        columns = jnp.concatenate(pieces, axis=-1).reshape(-1, 9 * channels)
        blocks.append(
            lax.dot_general(
                columns, flat_grad, (((0,), (0,)), ((), ())), preferred_element_type=jnp.float32
            )
        )
    return jnp.concatenate(blocks, axis=0)


def flip_kernel(kernel, inputs):
    outputs = kernel.shape[1]
    shaped = kernel.reshape(3, 3, 3, inputs, outputs)[::-1, ::-1, ::-1]
    return jnp.transpose(shaped, (0, 1, 2, 4, 3)).reshape(27 * outputs, inputs)


def silu_slope(value):
    sigmoid_v = jax.nn.sigmoid(value)
    return sigmoid_v * (1.0 + value * (1.0 - sigmoid_v))


def pool_columns(block):
    samples, extent_z, extent_x, extent_y, channels = block.shape
    shaped = block.reshape(samples, extent_z // 2, 2, extent_x // 2, 2, extent_y // 2, 2, channels)
    return jnp.transpose(shaped, (0, 1, 3, 5, 2, 4, 6, 7)).reshape(-1, 8 * channels)


def unpool_columns(flat, samples, extent_z, extent_x, extent_y, channels):
    shaped = flat.reshape(samples, extent_z // 2, extent_x // 2, extent_y // 2, 2, 2, 2, channels)
    return jnp.transpose(shaped, (0, 1, 4, 2, 5, 3, 6, 7)).reshape(
        samples, extent_z, extent_x, extent_y, channels
    )


def coarse_rim(block):
    return with_halo(block, (("gz", 1),), 1)


def coarse_grad_rim(block):
    return with_halo(block, (("gz", 1),), 1)


def coarse_kernel_total(partial_value):
    return lax.psum(partial_value.astype(jnp.bfloat16), "gz").astype(jnp.float32)


def per_device(volumes, cotangent, fine_kernel, down_kernel, coarse_kernel):
    samples, planes, xfine, packed = volumes.shape
    cfine = fine_kernel.shape[1]
    yfine = packed // cfine
    fine = volumes.reshape(samples, planes, xfine, yfine, cfine)
    fine_padded = pad_sides(with_halo(fine, (("gz", 1),), 1))
    fine_pre = convolve(fine_padded, fine_kernel)
    fine_act = jax.nn.silu(fine_pre).astype(jnp.bfloat16)
    pooled = pool_columns(fine_act)
    coarse_in = jnp.dot(pooled, down_kernel, preferred_element_type=jnp.float32).astype(
        jnp.bfloat16
    )
    coarse_in = coarse_in.reshape(samples, planes // 2, xfine // 2, yfine // 2, -1)
    coarse_framed = coarse_rim(coarse_in)
    gathered = pad_sides(lax.all_gather(coarse_framed, "grp", axis=0, tiled=True))
    coarse_pre = convolve(gathered, coarse_kernel)
    group, zcoarse, xcoarse, ycoarse, own_channels = coarse_pre.shape
    coarse_out = (
        jax.nn.silu(coarse_pre)
        .astype(jnp.bfloat16)
        .reshape(group, zcoarse, xcoarse * ycoarse, own_channels)
    )
    grad_shaped = cotangent.reshape(coarse_pre.shape).astype(jnp.float32)
    coarse_grad = (grad_shaped * silu_slope(coarse_pre)).astype(jnp.bfloat16)
    coarse_kg = coarse_kernel_total(kernel_gradient(gathered, coarse_grad))
    partial_value = convolve(
        pad_sides(coarse_grad_rim(coarse_grad)),
        flip_kernel(coarse_kernel, coarse_kernel.shape[0] // 27),
    )
    coarse_in_grad = lax.psum_scatter(
        partial_value.astype(jnp.bfloat16), "grp", scatter_dimension=0, tiled=True
    )
    flat_in_grad = coarse_in_grad.reshape(-1, coarse_in_grad.shape[-1])
    pooled_grad = jnp.dot(flat_in_grad, down_kernel.T, preferred_element_type=jnp.float32)
    fine_act_grad = unpool_columns(pooled_grad, samples, planes, xfine, yfine, cfine)
    down_kg = lax.dot_general(
        pooled, flat_in_grad, (((0,), (0,)), ((), ())), preferred_element_type=jnp.float32
    )
    fine_grad = (fine_act_grad * silu_slope(fine_pre)).astype(jnp.bfloat16)
    fine_kg = kernel_gradient(fine_padded, fine_grad)
    fine_kg, down_kg = lax.psum((fine_kg, down_kg), ("gz", "grp"))
    grad_padded = pad_sides(with_halo(fine_grad, (("gz", 1),), 1))
    volume_grad = convolve(grad_padded, flip_kernel(fine_kernel, cfine)).astype(jnp.bfloat16)
    volume_grad = volume_grad.reshape(samples, planes, xfine, packed)
    return (coarse_out, volume_grad, fine_kg, down_kg, coarse_kg)


def solution(mesh):
    in_specs = (P("grp", "gz", None, None), P(None, "gz", None, "grp"), P(), P(), P(None, "grp"))
    out_specs = (P(None, "gz", None, "grp"), P("grp", "gz", None, None), P(), P(), P(None, "grp"))
    return jax.shard_map(
        per_device, mesh=mesh, in_specs=in_specs, out_specs=out_specs, check_vma=False
    )
```

profile of v0, /device:TPU:1, one launch (start us, length us, event | category | flops | bytes accessed | tf_op | source)
XLA Modules:
  0.0 269.7 jit_solution(286053441385954328)
XLA Ops:
  9.2 4.7 %collective-permute-start = (bf16[1,1,16,16,64]{4,3,2,1,0:T(8,128)(2,1)S(1)}, bf16[1,1,16,16,64]{4,3,2,1,0:T(8,128)(2,1)S(1)}, u32[]{:S(2)}, u32[]{:S(2)}) collective-permute-start(bf16[1,1,16,16,64]{4,3,2,1,0:T(8,128)(2,1)S(1)} %get-tuple-element.108), channel_id=1, source_target_pairs={{0,4},{4,8},{8,12},{12,16},{16,20},{20,24},{24,28},{1,5},{5,9},{9,... | collective-permute-start | bytes 98312 | tf_op jit(solution)/shard_map/ppermute | solution.py:14
  13.9 1.9 collective-permute-start.1
  16.8 2.7 %collective-permute-done.1 = bf16[1,1,16,16,64]{4,3,2,1,0:T(8,128)(2,1)S(1)} collective-permute-done((bf16[1,1,16,16,64]{4,3,2,1,0:T(8,128)(2,1)S(1)}, bf16[1,1,16,16,64]{4,3,2,1,0:T(8,128)(2,1)S(1)}, u32[]{:S(2)}, u32[]{:S(2)}) %collective-permute-start.1) | collective-permute-done | bytes 32800 | tf_op jit(solution)/shard_map/ppermute | solution.py:15
  19.6 1.2 fusion.44
  24.7 1.3 convolution_add_fusion.3
  29.1 1.9 collective-permute-start.2
  31.0 2.4 collective-permute-start.3
  37.9 2.9 %rev.7 = bf16[3,3,3,64,64]{3,2,1,0,4:T(4,128)(2,1)} reverse(bf16[3,3,3,64,64]{3,2,1,0,4:T(4,128)(2,1)S(1)} %reshape.464), dimensions={0,1,2} | reverse | bytes 442368 | tf_op jit(solution)/shard_map/rev | solution.py:75
  40.8 7.0 %all_gather.3 = bf16[4,3,8,8,128]{4,3,2,0,1:T(8,128)(2,1)S(1)} all-gather(bf16[1,3,8,8,128]{4,3,2,0,1:T(8,128)(2,1)S(1)} %pad_maximum_fusion.5), channel_id=1, replica_groups=mesh['gz'=8,'grp'=4] {'grp'}, dimensions={0}, use_global_device_ids=true | all-gather | bytes 245760 | tf_op jit(solution)/shard_map/all_gather | solution.py:123
  51.1 1.5 multiply_convert_fusion.4
  56.4 4.9 %collective-permute-start.4 = (bf16[4,1,8,8,32]{4,3,2,0,1:T(8,128)(2,1)S(1)}, bf16[4,1,8,8,32]{4,3,2,0,1:T(8,128)(2,1)S(1)}, u32[]{:S(2)}, u32[]{:S(2)}) collective-permute-start(bf16[4,1,8,8,32]{4,3,2,0,1:T(8,128)(2,1)S(1)} %fusion.23), channel_id=1, source_target_pairs={{0,4},{4,8},{8,12},{12,16},{16,20},{20,24},{24,28},{1,5},{5,9},{9,... | collective-permute-start | bytes 49160 | tf_op jit(solution)/shard_map/ppermute | solution.py:14
  61.3 1.9 collective-permute-start.5
  64.0 2.9 %collective-permute-done.5 = bf16[4,1,8,8,32]{4,3,2,0,1:T(8,128)(2,1)S(1)} collective-permute-done((bf16[4,1,8,8,32]{4,3,2,0,1:T(8,128)(2,1)S(1)}, bf16[4,1,8,8,32]{4,3,2,0,1:T(8,128)(2,1)S(1)}, u32[]{:S(2)}, u32[]{:S(2)}) %collective-permute-start.5) | collective-permute-done | bytes 16416 | tf_op jit(solution)/shard_map/ppermute | solution.py:15
  77.3 40.1 %all-reduce.9.cloned.1.call-done = bf16[3456,32]{0,1:T(8,128)(2,1)} async-done(((bf16[3456,32]{0,1:T(8,128)(2,1)}), bf16[3456,32]{0,1:T(8,128)(2,1)}) %all-reduce.9.cloned.1.call-update) | async-done | bytes 221200 | tf_op jit(solution)/shard_map/psum | solution.py:106
  117.4 1.7 convert_element_type.157
  121.0 5.1 %collective-permute-start.6 = (bf16[1,1,16,16,64]{4,3,2,1,0:T(8,128)(2,1)S(1)}, bf16[1,1,16,16,64]{4,3,2,1,0:T(8,128)(2,1)S(1)}, u32[]{:S(2)}, u32[]{:S(2)}) collective-permute-start(bf16[1,1,16,16,64]{4,3,2,1,0:T(8,128)(2,1)S(1)} %get-tuple-element.104), channel_id=1, source_target_pairs={{0,4},{4,8},{8,12},{12,16},{16,20},{20,24},{24,28},{1,5},{5,9},{9,... | collective-permute-start | bytes 98312 | tf_op jit(solution)/shard_map/ppermute | solution.py:14
  126.1 2.1 collective-permute-start.7
  130.5 1.2 collective-permute-done.7
  133.7 1.6 copy.184
  135.3 1.6 copy.185
  136.9 1.6 copy.186
  138.5 1.6 copy.187
  149.0 110.6 %all-reduce.11.cloned.1.call-done = (f32[1728,64]{0,1:T(8,128)}, f32[512,128]{1,0:T(8,128)}) async-done(((f32[1728,64]{0,1:T(8,128)}, f32[512,128]{1,0:T(8,128)}), (f32[1728,64]{0,1:T(8,128)}, f32[512,128]{1,0:T(8,128)})) %all-reduce.11.cloned.1.call-update) | async-done | bytes 704528 | tf_op jit(solution)/shard_map/psum | solution.py:149
  259.7 1.9 copy.254
  (258 shorter events, 46.6 us)
Async XLA Ops:
  8.0 20.5 %copy-start = (bf16[512,128]{1,0:T(8,128)(2,1)S(1)}, bf16[512,128]{1,0:T(8,128)(2,1)}, u32[]{:S(2)}) copy-start(bf16[512,128]{1,0:T(8,128)(2,1)} %param.8) | copy-start | bytes 393220
  8.0 109.4 %all-reduce.9.cloned.1.call-start = ((), (), s32[]{:S(2)}) async-start(), calls=%async_computation.1 | async-start | bytes 442368 | tf_op jit(solution)/shard_map/psum | solution.py:106
  8.1 7.8 %copy-start.47 = (bf16[1,2,16,1024]{3,2,1,0:T(8,128)(2,1)S(1)}, bf16[1,2,16,1024]{3,2,1,0:T(8,128)(2,1)}, u32[]{:S(2)}) copy-start(bf16[1,2,16,1024]{3,2,1,0:T(8,128)(2,1)} %param.5) | copy-start | bytes 196612
  9.1 6.8 %copy-start.21 = (bf16[3456,32]{0,1:T(8,128)(2,1)S(1)}, bf16[3456,32]{0,1:T(8,128)(2,1)}, u32[]{:S(2)}) copy-start(bf16[3456,32]{0,1:T(8,128)(2,1)} %param.9) | copy-start | bytes 663556
  9.2 7.6 %collective-permute-start = (bf16[1,1,16,16,64]{4,3,2,1,0:T(8,128)(2,1)S(1)}, bf16[1,1,16,16,64]{4,3,2,1,0:T(8,128)(2,1)S(1)}, u32[]{:S(2)}, u32[]{:S(2)}) collective-permute-start(bf16[1,1,16,16,64]{4,3,2,1,0:T(8,128)(2,1)S(1)} %get-tuple-element.108), channel_id=1, source_target_pairs={{0,4},{4,8},{8,12},{12,16},{16,20},{20,24},{24,28},{1,5},{5,9},{9,... | collective-permute-start | bytes 98312 | tf_op jit(solution)/shard_map/ppermute | solution.py:14
  13.9 5.6 %collective-permute-start.1 = (bf16[1,1,16,16,64]{4,3,2,1,0:T(8,128)(2,1)S(1)}, bf16[1,1,16,16,64]{4,3,2,1,0:T(8,128)(2,1)S(1)}, u32[]{:S(2)}, u32[]{:S(2)}) collective-permute-start(bf16[1,1,16,16,64]{4,3,2,1,0:T(8,128)(2,1)S(1)} %get-tuple-element.109), channel_id=1, source_target_pairs={{4,0},{8,4},{12,8},{16,12},{20,16},{24,20},{28,24},{5,1},{9,5},{13... | collective-permute-start | bytes 98312 | tf_op jit(solution)/shard_map/ppermute | solution.py:15
  24.2 1.9 copy-start.35
  24.7 1.4 copy-start.28
  29.1 11.7 %collective-permute-start.2 = (bf16[1,1,8,8,128]{4,3,2,0,1:T(8,128)(2,1)S(1)}, bf16[1,1,8,8,128]{4,3,2,0,1:T(8,128)(2,1)S(1)}, u32[]{:S(2)}, u32[]{:S(2)}) collective-permute-start(bf16[1,1,8,8,128]{4,3,2,0,1:T(8,128)(2,1)S(1)} %fusion.6), channel_id=1, source_target_pairs={{0,4},{4,8},{8,12},{12,16},{16,20},{20,24},{24,28},{1,5},{5,9},{9,... | collective-permute-start | bytes 49160 | tf_op jit(solution)/shard_map/ppermute | solution.py:14
  31.0 9.8 %collective-permute-start.3 = (bf16[1,1,8,8,128]{4,3,2,0,1:T(8,128)(2,1)S(1)}, bf16[1,1,8,8,128]{4,3,2,0,1:T(8,128)(2,1)S(1)}, u32[]{:S(2)}, u32[]{:S(2)}) collective-permute-start(bf16[1,1,8,8,128]{4,3,2,0,1:T(8,128)(2,1)S(1)} %fusion.6), channel_id=1, source_target_pairs={{4,0},{8,4},{12,8},{16,12},{20,16},{24,20},{28,24},{5,1},{9,5},{13... | collective-permute-start | bytes 49160 | tf_op jit(solution)/shard_map/ppermute | solution.py:15
  56.3 6.9 %copy-start.44 = (bf16[1152,32]{0,1:T(8,128)(2,1)S(1)}, bf16[1152,32]{0,1:T(8,128)(2,1)}, u32[]{:S(2)}) copy-start(bf16[1152,32]{0,1:T(8,128)(2,1)} %fusion) | copy-start | bytes 221188
  56.4 7.6 %collective-permute-start.4 = (bf16[4,1,8,8,32]{4,3,2,0,1:T(8,128)(2,1)S(1)}, bf16[4,1,8,8,32]{4,3,2,0,1:T(8,128)(2,1)S(1)}, u32[]{:S(2)}, u32[]{:S(2)}) collective-permute-start(bf16[4,1,8,8,32]{4,3,2,0,1:T(8,128)(2,1)S(1)} %fusion.23), channel_id=1, source_target_pairs={{0,4},{4,8},{8,12},{12,16},{16,20},{20,24},{24,28},{1,5},{5,9},{9,... | collective-permute-start | bytes 49160 | tf_op jit(solution)/shard_map/ppermute | solution.py:14
  61.3 5.6 %collective-permute-start.5 = (bf16[4,1,8,8,32]{4,3,2,0,1:T(8,128)(2,1)S(1)}, bf16[4,1,8,8,32]{4,3,2,0,1:T(8,128)(2,1)S(1)}, u32[]{:S(2)}, u32[]{:S(2)}) collective-permute-start(bf16[4,1,8,8,32]{4,3,2,0,1:T(8,128)(2,1)S(1)} %fusion.23), channel_id=1, source_target_pairs={{4,0},{8,4},{12,8},{16,12},{20,16},{24,20},{28,24},{5,1},{9,5},{13... | collective-permute-start | bytes 49160 | tf_op jit(solution)/shard_map/ppermute | solution.py:15
  64.0 55.1 %reduce-scatter.4.cloned.1.call-start = ((), (), s32[]{:S(2)}) async-start(), calls=%async_computation.2 | async-start | bytes 81920
  72.4 1.8 copy-start.3
  74.1 185.6 %all-reduce.11.cloned.1.call-start = ((), (), s32[]{:S(2)}) async-start(), calls=%async_computation.3 | async-start | bytes 1441792 | tf_op jit(solution)/shard_map/psum | solution.py:149
  74.4 2.1 copy-start.15
  74.4 2.1 copy-start.17
  77.3 41.8 %copy-start.2 = (f32[512,64]{1,0:T(8,128)S(1)}, f32[512,64]{1,0:T(8,128)}, u32[]{:S(2)}) copy-start(f32[512,64]{1,0:T(8,128)} %copy-done.1) | copy-start | bytes 393220
  121.0 7.2 %copy-start.24 = (bf16[64,512]{1,0:T(8,128)(2,1)S(1)}, bf16[64,512]{1,0:T(8,128)(2,1)}, u32[]{:S(2)}) copy-start(bf16[64,512]{1,0:T(8,128)(2,1)} %copy-done.23) | copy-start | bytes 196612
  121.0 7.2 %copy-start.59 = (bf16[1,1,8,8,128]{4,3,2,1,0:T(8,128)(2,1)S(1)}, bf16[1,1,8,8,128]{4,3,2,1,0:T(8,128)(2,1)}, u32[]{:S(2)}) copy-start(bf16[1,1,8,8,128]{4,3,2,1,0:T(8,128)(2,1)} %reduce-scatter.4.cloned.1.call-done) | copy-start | bytes 49156
  121.0 9.4 %collective-permute-start.6 = (bf16[1,1,16,16,64]{4,3,2,1,0:T(8,128)(2,1)S(1)}, bf16[1,1,16,16,64]{4,3,2,1,0:T(8,128)(2,1)S(1)}, u32[]{:S(2)}, u32[]{:S(2)}) collective-permute-start(bf16[1,1,16,16,64]{4,3,2,1,0:T(8,128)(2,1)S(1)} %get-tuple-element.104), channel_id=1, source_target_pairs={{0,4},{4,8},{8,12},{12,16},{16,20},{20,24},{24,28},{1,5},{5,9},{9,... | collective-permute-start | bytes 98312 | tf_op jit(solution)/shard_map/ppermute | solution.py:14
  126.1 5.6 %collective-permute-start.7 = (bf16[1,1,16,16,64]{4,3,2,1,0:T(8,128)(2,1)S(1)}, bf16[1,1,16,16,64]{4,3,2,1,0:T(8,128)(2,1)S(1)}, u32[]{:S(2)}, u32[]{:S(2)}) collective-permute-start(bf16[1,1,16,16,64]{4,3,2,1,0:T(8,128)(2,1)S(1)} %get-tuple-element.105), channel_id=1, source_target_pairs={{4,0},{8,4},{12,8},{16,12},{20,16},{24,20},{28,24},{5,1},{9,5},{13... | collective-permute-start | bytes 98312 | tf_op jit(solution)/shard_map/ppermute | solution.py:15
  259.7 1.9 copy-start.52
  (47 other events, 45.4 us)
Sparse Core Ops, SparseCore 0:
  64.1 53.2 all-reduce.8
Sparse Core Ops, SparseCore 1:
  74.2 22.2 reduce-scatter.3
  130.5 129.1 all-reduce.10
where the time goes:
time: 271 us; the launch traced here: 270 us
  waiting for transfers between devices  158 us (58%)
  local copies, waits for them, and re-layouts  48.7 us (18%)
  starting transfers between devices  25.1 us (9%)
  between operations  16.6 us (6%)
  matrix products  9.78 us (4%)
  blocking collectives  6.97 us (3%)
  other arithmetic  4.97 us (2%)
    psum x1, waiting for transfers between devices, per_device(): fine_kg, down_kg = lax.psum((fine_kg, down_kg), ('gz', 'grp'))  111 us
    psum x1, waiting for transfers between devices, coarse_kernel_total(): lax.psum(partial_value.astype(jnp.bfloat16), 'gz').astype(jnp.float32)  40.1 us
    unnamed x156, local copies, waits for them, and re-layouts  19.7 us
    ppermute x4, starting transfers between devices, with_halo(): before = lax.ppermute(last, axis, up)  16.6 us
    concatenate x30, local copies, waits for them, and re-layouts, convolve(): columns = jnp.concatenate(pieces, axis=-1).reshape(-1, 9 * channels)  11.2 us
    ppermute x4, starting transfers between devices, with_halo(): after = lax.ppermute(initial, axis, down)  8.34 us
    all_gather x1, blocking collectives, per_device(): lax.all_gather(coarse_framed, 'grp', axis=0, tiled=True)  6.97 us
    ppermute x4, waiting for transfers between devices, with_halo(): after = lax.ppermute(initial, axis, down)  6.81 us
  transfers between devices with their start and end apart: 11, of which 5 were waited for; matrix products, arithmetic and copies ran while one was open for 11% of the time, Pallas kernels for 0%

commit v1 on v0

--- a/solution.py
+++ b/solution.py
@@ -1,6 +1,10 @@
+import functools
+
 import jax
 import jax.numpy as jnp
 from jax import lax
+from jax.experimental import pallas as pl
+from jax.experimental.pallas import tpu as pltpu
 from jax.sharding import PartitionSpec as P
 
 
@@ -102,8 +106,204 @@
     return with_halo(block, (("gz", 1),), 1)
 
 
-def coarse_kernel_total(partial_value):
-    return lax.psum(partial_value.astype(jnp.bfloat16), "gz").astype(jnp.float32)
+MESH = pl.DeviceIdType.MESH
+
+
+def exchange(src, dst, sends, recvs, slot, peer):
+    return pltpu.make_async_remote_copy(
+        src_ref=src,
+        dst_ref=dst,
+        send_sem=sends.at[slot],
+        recv_sem=recvs.at[slot],
+        device_id=peer,
+        device_id_type=MESH,
+    )
+
+
+def totals_kernel(
+    groups,
+    slabs,
+    both_ref,
+    slab_ref,
+    both_out,
+    slab_out,
+    grp_in,
+    grp_sum,
+    gz_in,
+    both_all,
+    slab_in,
+    slab_all,
+    grp_send,
+    grp_recv,
+    gz_send,
+    gz_recv,
+    slab_send,
+    slab_recv,
+):
+    z = lax.axis_index("gz")
+    g = lax.axis_index("grp")
+
+    def at_gz(step):
+        return lax.rem(z + step, slabs)
+
+    def at_grp(step):
+        return lax.rem(g + step, groups)
+
+    barrier = pltpu.get_barrier_semaphore()
+    for step in range(1, slabs):
+        pl.semaphore_signal(barrier, inc=1, device_id=(at_gz(step), g), device_id_type=MESH)
+    for step in range(1, groups):
+        pl.semaphore_signal(barrier, inc=1, device_id=(z, at_grp(step)), device_id_type=MESH)
+    pl.semaphore_wait(barrier, slabs + groups - 2)
+
+    def run(copies):
+        for copy in copies:
+            copy.start()
+        return copies
+
+    def finish(copies):
+        for copy in copies:
+            copy.wait()
+
+    first = run(
+        [
+            exchange(
+                both_ref.at[at_grp(k)], grp_in.at[k - 1], grp_send.at[0], grp_recv.at[0], k - 1,
+                (z, at_grp(k)),
+            )
+            for k in range(1, groups)
+        ]
+    )
+    slab_first = run(
+        [
+            exchange(
+                slab_ref.at[at_gz(k)], slab_in.at[k - 1], slab_send.at[0], slab_recv.at[0], k - 1,
+                (at_gz(k), g),
+            )
+            for k in range(1, slabs)
+        ]
+    )
+    finish(first)
+    total = both_ref[g].astype(jnp.float32)
+    for k in range(groups - 1):
+        total = total + grp_in[k].astype(jnp.float32)
+    grp_sum[...] = total.astype(jnp.bfloat16)
+    second = run(
+        [
+            exchange(
+                grp_sum.at[at_gz(k)], gz_in.at[k - 1], gz_send.at[0], gz_recv.at[0], k - 1,
+                (at_gz(k), g),
+            )
+            for k in range(1, slabs)
+        ]
+    )
+    finish(slab_first)
+    slab_total = slab_ref[z].astype(jnp.float32)
+    for k in range(slabs - 1):
+        slab_total = slab_total + slab_in[k].astype(jnp.float32)
+    slab_all[z] = slab_total.astype(jnp.bfloat16)
+    finish(second)
+    own = grp_sum[z].astype(jnp.float32)
+    for k in range(slabs - 1):
+        own = own + gz_in[k].astype(jnp.float32)
+    both_all[g, z] = own.astype(jnp.bfloat16)
+    third = run(
+        [
+            exchange(
+                both_all.at[g, z], both_all.at[g, z], gz_send.at[1], gz_recv.at[1], k - 1,
+                (at_gz(k), g),
+            )
+            for k in range(1, slabs)
+        ]
+    )
+    slab_second = run(
+        [
+            exchange(
+                slab_all.at[z], slab_all.at[z], slab_send.at[1], slab_recv.at[1], k - 1,
+                (at_gz(k), g),
+            )
+            for k in range(1, slabs)
+        ]
+    )
+    finish(third)
+    fourth = run(
+        [
+            exchange(
+                both_all.at[g], both_all.at[g], grp_send.at[1], grp_recv.at[1], k - 1,
+                (z, at_grp(k)),
+            )
+            for k in range(1, groups)
+        ]
+    )
+    finish(slab_second)
+    slab_out[...] = slab_all[...].astype(jnp.float32)
+    finish(fourth)
+    both_out[...] = both_all[...].astype(jnp.float32)
+
+
+def to_rows(array):
+    fold = max(1, 128 // array.shape[1])
+    rows = array.shape[0] // fold
+    parts = [array[k * rows : (k + 1) * rows] for k in range(fold)]
+    return jnp.concatenate(parts, axis=1) if fold > 1 else array
+
+
+def from_rows(rows, shape):
+    fold = max(1, 128 // shape[1])
+    width = shape[1]
+    parts = [rows[:, k * width : (k + 1) * width] for k in range(fold)]
+    return jnp.concatenate(parts, axis=0) if fold > 1 else rows
+
+
+def pad_rows(rows, pieces):
+    depth = -(-rows.shape[0] // (pieces * 16)) * 16
+    return jnp.pad(rows, ((0, pieces * depth - rows.shape[0]), (0, 0))), depth
+
+
+def kernel_totals(fine_kg, down_kg, coarse_kg):
+    slabs, groups = lax.axis_size("gz"), lax.axis_size("grp")
+    fine_rows = to_rows(fine_kg.astype(jnp.bfloat16))
+    down_rows = to_rows(down_kg.astype(jnp.bfloat16))
+    coarse_rows = to_rows(coarse_kg.astype(jnp.bfloat16))
+    fine_count, down_count, coarse_count = (
+        fine_rows.shape[0], down_rows.shape[0], coarse_rows.shape[0],
+    )
+    both, depth = pad_rows(jnp.concatenate([fine_rows, down_rows], axis=0), slabs * groups)
+    slab, slab_depth = pad_rows(coarse_rows, slabs)
+    both = both.reshape(groups, slabs, depth, 128)
+    slab = slab.reshape(slabs, slab_depth, 128)
+    vmem = pl.BlockSpec(memory_space=pltpu.VMEM)
+    dma = pltpu.SemaphoreType.DMA
+    both, slab = pl.pallas_call(
+        functools.partial(totals_kernel, groups, slabs),
+        out_shape=(
+            jax.ShapeDtypeStruct(both.shape, jnp.float32),
+            jax.ShapeDtypeStruct(slab.shape, jnp.float32),
+        ),
+        in_specs=[vmem, vmem],
+        out_specs=(vmem, vmem),
+        scratch_shapes=[
+            pltpu.VMEM((groups - 1, slabs, depth, 128), jnp.bfloat16),
+            pltpu.VMEM((slabs, depth, 128), jnp.bfloat16),
+            pltpu.VMEM((slabs - 1, depth, 128), jnp.bfloat16),
+            pltpu.VMEM(both.shape, jnp.bfloat16),
+            pltpu.VMEM((slabs - 1, slab_depth, 128), jnp.bfloat16),
+            pltpu.VMEM(slab.shape, jnp.bfloat16),
+            dma((2, groups - 1)),
+            dma((2, groups - 1)),
+            dma((2, slabs - 1)),
+            dma((2, slabs - 1)),
+            dma((2, slabs - 1)),
+            dma((2, slabs - 1)),
+        ],
+        compiler_params=pltpu.CompilerParams(collective_id=0, has_side_effects=True),
+    )(both, slab)
+    both, slab = both.reshape(-1, 128), slab.reshape(-1, 128)
+    return (
+        from_rows(both[:fine_count], fine_kg.shape),
+        from_rows(both[fine_count : fine_count + down_count], down_kg.shape),
+        from_rows(slab[:coarse_count], coarse_kg.shape),
+    )
 
 
 def per_device(volumes, cotangent, fine_kernel, down_kernel, coarse_kernel):
@@ -130,7 +330,7 @@
     )
     grad_shaped = cotangent.reshape(coarse_pre.shape).astype(jnp.float32)
     coarse_grad = (grad_shaped * silu_slope(coarse_pre)).astype(jnp.bfloat16)
-    coarse_kg = coarse_kernel_total(kernel_gradient(gathered, coarse_grad))
+    coarse_kg = kernel_gradient(gathered, coarse_grad)
     partial_value = convolve(
         pad_sides(coarse_grad_rim(coarse_grad)),
         flip_kernel(coarse_kernel, coarse_kernel.shape[0] // 27),
@@ -146,7 +346,7 @@
     )
     fine_grad = (fine_act_grad * silu_slope(fine_pre)).astype(jnp.bfloat16)
     fine_kg = kernel_gradient(fine_padded, fine_grad)
-    fine_kg, down_kg = lax.psum((fine_kg, down_kg), ("gz", "grp"))
+    fine_kg, down_kg, coarse_kg = kernel_totals(fine_kg, down_kg, coarse_kg)
     grad_padded = pad_sides(with_halo(fine_grad, (("gz", 1),), 1))
     volume_grad = convolve(grad_padded, flip_kernel(fine_kernel, cfine)).astype(jnp.bfloat16)
     volume_grad = volume_grad.reshape(samples, planes, xfine, packed)

time: 271 us -> 183 us (0.68)
  waiting for transfers between devices: 158 us -> 21.7 us
  Pallas kernels: 0 us -> 28 us
  local copies, waits for them, and re-layouts: 48.7 us -> 65.5 us
    psum x2 -> x0, waiting for transfers between devices: 151 us -> none  [the longest x1 111 us: per_device(): fine_kg, down_kg = lax.psum((fine_kg, down_kg), ('gz', 'grp'))]
    pallas_call x0 -> x1, Pallas kernels: none -> 28 us  [kernel_totals(): pl.pallas_call(functools.partial(totals_kernel, groups, slabs), out_shape...]
    unnamed x4 -> x2, waiting for transfers between devices: 0.05 us -> 21.1 us
    concatenate x30, local copies, waits for them, and re-layouts: 11.2 us -> 20.8 us  [convolve(): columns = jnp.concatenate(pieces, axis=-1).reshape(-1, 9 * channels)]
    ppermute x4, waiting for transfers between devices: 6.81 us -> 0.64 us  [with_halo(): after = lax.ppermute(initial, axis, down)]
    slice x0 -> x6, local copies, waits for them, and re-layouts: none -> 3.98 us  [the longest x2 3.17 us: from_rows(): parts = [rows[:, k * width:(k + 1) * width] for k in range(fold)]]
    unnamed x156 -> x133, local copies, waits for them, and re-layouts: 19.7 us -> 19.3 us
  transfers between devices with their start and end apart: 11 -> 9, of which waited for: 5 -> 2; matrix products, arithmetic and copies ran while one was open for 11% -> 10% of each run, Pallas kernels for 0% -> 0%
where the time goes in v1:
time: 183 us; the launch traced here: 181 us
  local copies, waits for them, and re-layouts  65.5 us (36%)
  Pallas kernels  28 us (15%)
  starting transfers between devices  25.2 us (14%)
  waiting for transfers between devices  21.7 us (12%)
  between operations  15 us (8%)
  matrix products  12.2 us (7%)
  blocking collectives  6.7 us (4%)
  other arithmetic  6.23 us (3%)
    pallas_call x1, Pallas kernels, kernel_totals(): pl.pallas_call(functools.partial(totals_kernel, groups, slabs), out_shape...  28 us
    unnamed x2, waiting for transfers between devices  21.1 us
    concatenate x30, local copies, waits for them, and re-layouts, convolve(): columns = jnp.concatenate(pieces, axis=-1).reshape(-1, 9 * channels)  20.8 us
    unnamed x133, local copies, waits for them, and re-layouts  19.3 us
    ppermute x4, starting transfers between devices, with_halo(): before = lax.ppermute(last, axis, up)  17.3 us
    dot_general x12, matrix products, convolve(): partial_value = jnp.dot(columns, rows, preferred_element_type=jnp.float32)  8 us
    ppermute x4, starting transfers between devices, with_halo(): after = lax.ppermute(initial, axis, down)  7.86 us
    all_gather x1, blocking collectives, per_device(): lax.all_gather(coarse_framed, 'grp', axis=0, tiled=True)  6.7 us
  transfers between devices with their start and end apart: 9, of which 2 were waited for; matrix products, arithmetic and copies ran while one was open for 10% of the time, Pallas kernels for 0%

profile of v1, /device:TPU:1, one launch (start us, length us, event | category | flops | bytes accessed | tf_op | source)
XLA Modules:
  0.0 180.6 jit_solution(6574545637543531881)
XLA Ops:
  8.3 4.6 %collective-permute-start = (bf16[1,1,16,16,64]{4,3,2,1,0:T(8,128)(2,1)S(1)}, bf16[1,1,16,16,64]{4,3,2,1,0:T(8,128)(2,1)S(1)}, u32[]{:S(2)}, u32[]{:S(2)}) collective-permute-start(bf16[1,1,16,16,64]{4,3,2,1,0:T(8,128)(2,1)S(1)} %get-tuple-element.131), channel_id=1, source_target_pairs={{0,4},{4,8},{8,12},{12,16},{16,20},{20,24},{24,28},{1,5},{5,9},{9,... | collective-permute-start | bytes 98312 | tf_op jit(solution)/shard_map/ppermute | solution.py:18
  12.9 1.9 %collective-permute-start.1 = (bf16[1,1,16,16,64]{4,3,2,1,0:T(8,128)(2,1)S(1)}, bf16[1,1,16,16,64]{4,3,2,1,0:T(8,128)(2,1)S(1)}, u32[]{:S(2)}, u32[]{:S(2)}) collective-permute-start(bf16[1,1,16,16,64]{4,3,2,1,0:T(8,128)(2,1)S(1)} %get-tuple-element.132), channel_id=1, source_target_pairs={{4,0},{8,4},{12,8},{16,12},{20,16},{24,20},{28,24},{5,1},{9,5},{13... | collective-permute-start | bytes 98312 | tf_op jit(solution)/shard_map/ppermute | solution.py:19
  15.2 1.7 rev.7
  22.4 1.3 concatenate.154
  23.7 1.9 %convolution_add_fusion.3 = f32[512,64]{0,1:T(8,128)} fusion(f32[512,64]{0,1:T(8,128)} %fusion.38, bf16[512,576]{1,0:T(8,128)(2,1)S(1)} %bitcast.186, bf16[1728,64]{0,1:T(8,128)(2,1)S(1)} %copy-done.6), kind=kOutput, calls=%fused_computation.46 | convolution fusion | flops 37781504 | bytes 999424 | tf_op jit(solution)/shard_map/dot_general | solution.py:46
  25.6 1.4 concatenate.166
  29.9 3.6 %collective-permute-start.2 = (bf16[1,1,8,8,128]{4,3,2,0,1:T(8,128)(2,1)S(1)}, bf16[1,1,8,8,128]{4,3,2,0,1:T(8,128)(2,1)S(1)}, u32[]{:S(2)}, u32[]{:S(2)}) collective-permute-start(bf16[1,1,8,8,128]{4,3,2,0,1:T(8,128)(2,1)S(1)} %fusion.9), channel_id=1, source_target_pairs={{0,4},{4,8},{8,12},{12,16},{16,20},{20,24},{24,28},{1,5},{5,9},{9,... | collective-permute-start | bytes 49160 | tf_op jit(solution)/shard_map/ppermute | solution.py:18
  33.6 1.9 %collective-permute-start.3 = (bf16[1,1,8,8,128]{4,3,2,0,1:T(8,128)(2,1)S(1)}, bf16[1,1,8,8,128]{4,3,2,0,1:T(8,128)(2,1)S(1)}, u32[]{:S(2)}, u32[]{:S(2)}) collective-permute-start(bf16[1,1,8,8,128]{4,3,2,0,1:T(8,128)(2,1)S(1)} %fusion.9), channel_id=1, source_target_pairs={{4,0},{8,4},{12,8},{16,12},{20,16},{24,20},{28,24},{5,1},{9,5},{13... | collective-permute-start | bytes 49160 | tf_op jit(solution)/shard_map/ppermute | solution.py:19
  43.2 6.7 %all_gather.3 = bf16[4,3,8,8,128]{4,3,2,0,1:T(8,128)(2,1)S(1)} all-gather(bf16[1,3,8,8,128]{4,3,2,0,1:T(8,128)(2,1)S(1)} %pad_maximum_fusion.8), channel_id=1, replica_groups=mesh['gz'=8,'grp'=4] {'grp'}, dimensions={0}, use_global_device_ids=true | all-gather | bytes 245760 | tf_op jit(solution)/shard_map/all_gather | solution.py:323
  54.0 1.7 fusion.35
  55.6 5.7 %collective-permute-start.4 = (bf16[4,1,8,8,32]{4,3,2,0,1:T(8,128)(2,1)}, bf16[4,1,8,8,32]{4,3,2,0,1:T(8,128)(2,1)}, u32[]{:S(2)}, u32[]{:S(2)}) collective-permute-start(bf16[4,1,8,8,32]{4,3,2,0,1:T(8,128)(2,1)} %fusion.35), channel_id=1, source_target_pairs={{0,4},{4,8},{8,12},{12,16},{16,20},{20,24},{24,28},{1,5},{5,9},{9,... | collective-permute-start | bytes 49160 | tf_op jit(solution)/shard_map/ppermute | solution.py:18
  61.3 1.9 %collective-permute-start.5 = (bf16[4,1,8,8,32]{4,3,2,0,1:T(8,128)(2,1)}, bf16[4,1,8,8,32]{4,3,2,0,1:T(8,128)(2,1)}, u32[]{:S(2)}, u32[]{:S(2)}) collective-permute-start(bf16[4,1,8,8,32]{4,3,2,0,1:T(8,128)(2,1)} %fusion.35), channel_id=1, source_target_pairs={{4,0},{8,4},{12,8},{16,12},{20,16},{24,20},{28,24},{5,1},{9,5},{13... | collective-permute-start | bytes 49160 | tf_op jit(solution)/shard_map/ppermute | solution.py:19
  69.8 1.5 copy.199
  71.3 1.3 constant_dynamic-update-slice_fusion.35
  72.7 1.5 copy.200
  87.6 21.1 %reduce-scatter.4.cloned.1.call-done = bf16[1,1,8,8,128]{4,3,2,1,0:T(8,128)(2,1)} async-done(((bf16[4,1,8,8,128]{4,3,2,1,0:T(8,128)(2,1)}), bf16[1,1,8,8,128]{4,3,2,1,0:T(8,128)(2,1)}) %reduce-scatter.4.cloned.1.call-update) | async-done | bytes 16400
  113.0 28.0 %shard_map.92 = (f32[4,8,48,128]{3,2,1,0:T(8,128)}, f32[8,112,128]{2,1,0:T(8,128)}) custom-call(bf16[4,8,48,128]{3,2,1,0:T(8,128)(2,1)} %bitcast.204, bf16[8,112,128]{2,1,0:T(8,128)(2,1)} %bitcast.214), custom_call_target="tpu_custom_call" | custom-call | tf_op jit(solution)/shard_map/pallas_call | solution.py:277
  141.1 3.0 %fusion.54 = (f32[864,32]{1,0:T(8,128)S(1)}, f32[864,32]{1,0:T(8,128)S(1)}, f32[864,32]{1,0:T(8,128)}, f32[864,32]{1,0:T(8,128)S(1)}) fusion(f32[896,128]{1,0:T(8,128)} %bitcast.185), kind=kLoop, calls=%fused_computation.174 | loop fusion | bytes 884736 | tf_op jit(solution)/shard_map/slice | solution.py:254
  145.2 3.4 %collective-permute-start.6 = (bf16[1,1,16,16,64]{4,3,2,1,0:T(8,128)(2,1)}, bf16[1,1,16,16,64]{4,3,2,1,0:T(8,128)(2,1)S(1)}, u32[]{:S(2)}, u32[]{:S(2)}) collective-permute-start(bf16[1,1,16,16,64]{4,3,2,1,0:T(8,128)(2,1)} %get-tuple-element.127), channel_id=1, source_target_pairs={{0,4},{4,8},{8,12},{12,16},{16,20},{20,24},{24,28},{1,5},{5,9},{9,... | collective-permute-start | bytes 98312 | tf_op jit(solution)/shard_map/ppermute | solution.py:18
  148.6 2.1 %collective-permute-start.7 = (bf16[1,1,16,16,64]{4,3,2,1,0:T(8,128)(2,1)}, bf16[1,1,16,16,64]{4,3,2,1,0:T(8,128)(2,1)}, u32[]{:S(2)}, u32[]{:S(2)}) collective-permute-start(bf16[1,1,16,16,64]{4,3,2,1,0:T(8,128)(2,1)} %get-tuple-element.128), channel_id=1, source_target_pairs={{4,0},{8,4},{12,8},{16,12},{20,16},{24,20},{28,24},{5,1},{9,5},{13... | collective-permute-start | bytes 98312 | tf_op jit(solution)/shard_map/ppermute | solution.py:19
  157.6 1.6 copy.216
  159.2 1.6 copy.217
  160.8 1.6 copy.218
  162.4 1.6 copy.219
  (239 shorter events, 62.8 us)
Async XLA Ops:
  7.2 22.1 %copy-start = (bf16[512,128]{1,0:T(8,128)(2,1)S(1)}, bf16[512,128]{1,0:T(8,128)(2,1)}, u32[]{:S(2)}) copy-start(bf16[512,128]{1,0:T(8,128)(2,1)} %param.8) | copy-start | bytes 393220
  7.2 7.7 %copy-start.6 = (bf16[1728,64]{0,1:T(8,128)(2,1)S(1)}, bf16[1728,64]{0,1:T(8,128)(2,1)}, u32[]{:S(2)}) copy-start(bf16[1728,64]{0,1:T(8,128)(2,1)} %param.7) | copy-start | bytes 663556
  7.2 101.4 %reduce-scatter.4.cloned.1.call-start = ((), (), s32[]{:S(2)}) async-start(), calls=%async_computation.1 | async-start | bytes 81920
  8.3 10.5 %collective-permute-start = (bf16[1,1,16,16,64]{4,3,2,1,0:T(8,128)(2,1)S(1)}, bf16[1,1,16,16,64]{4,3,2,1,0:T(8,128)(2,1)S(1)}, u32[]{:S(2)}, u32[]{:S(2)}) collective-permute-start(bf16[1,1,16,16,64]{4,3,2,1,0:T(8,128)(2,1)S(1)} %get-tuple-element.131), channel_id=1, source_target_pairs={{0,4},{4,8},{8,12},{12,16},{16,20},{20,24},{24,28},{1,5},{5,9},{9,... | collective-permute-start | bytes 98312 | tf_op jit(solution)/shard_map/ppermute | solution.py:18
  12.9 5.9 %collective-permute-start.1 = (bf16[1,1,16,16,64]{4,3,2,1,0:T(8,128)(2,1)S(1)}, bf16[1,1,16,16,64]{4,3,2,1,0:T(8,128)(2,1)S(1)}, u32[]{:S(2)}, u32[]{:S(2)}) collective-permute-start(bf16[1,1,16,16,64]{4,3,2,1,0:T(8,128)(2,1)S(1)} %get-tuple-element.132), channel_id=1, source_target_pairs={{4,0},{8,4},{12,8},{16,12},{20,16},{24,20},{28,24},{5,1},{9,5},{13... | collective-permute-start | bytes 98312 | tf_op jit(solution)/shard_map/ppermute | solution.py:19
  17.0 1.1 copy-start.7
  21.3 1.0 copy-start.34
  23.7 1.9 %copy-start.18 = (bf16[1,2,16,16,64]{4,3,2,1,0:T(8,128)(2,1)S(1)}, bf16[1,2,16,16,64]{4,3,2,1,0:T(8,128)(2,1)}, u32[]{:S(2)}) copy-start(bf16[1,2,16,16,64]{4,3,2,1,0:T(8,128)(2,1)} %get-tuple-element.91) | copy-start | bytes 196612
  29.9 13.2 %collective-permute-start.2 = (bf16[1,1,8,8,128]{4,3,2,0,1:T(8,128)(2,1)S(1)}, bf16[1,1,8,8,128]{4,3,2,0,1:T(8,128)(2,1)S(1)}, u32[]{:S(2)}, u32[]{:S(2)}) collective-permute-start(bf16[1,1,8,8,128]{4,3,2,0,1:T(8,128)(2,1)S(1)} %fusion.9), channel_id=1, source_target_pairs={{0,4},{4,8},{8,12},{12,16},{16,20},{20,24},{24,28},{1,5},{5,9},{9,... | collective-permute-start | bytes 49160 | tf_op jit(solution)/shard_map/ppermute | solution.py:18
  33.6 9.6 %collective-permute-start.3 = (bf16[1,1,8,8,128]{4,3,2,0,1:T(8,128)(2,1)S(1)}, bf16[1,1,8,8,128]{4,3,2,0,1:T(8,128)(2,1)S(1)}, u32[]{:S(2)}, u32[]{:S(2)}) collective-permute-start(bf16[1,1,8,8,128]{4,3,2,0,1:T(8,128)(2,1)S(1)} %fusion.9), channel_id=1, source_target_pairs={{4,0},{8,4},{12,8},{16,12},{20,16},{24,20},{28,24},{5,1},{9,5},{13... | collective-permute-start | bytes 49160 | tf_op jit(solution)/shard_map/ppermute | solution.py:19
  38.4 1.3 copy-start.11
  39.6 1.0 copy-start.10
  40.3 1.0 copy-start.9
  54.0 9.3 %copy-start.24 = (bf16[4,1,64,32]{2,3,1,0:T(8,128)(2,1)S(1)}, bf16[4,1,64,32]{2,3,1,0:T(8,128)(2,1)}, u32[]{:S(2)}) copy-start(bf16[4,1,64,32]{2,3,1,0:T(8,128)(2,1)} %param.6) | copy-start | bytes 49156
  54.0 9.3 %copy-start.32 = (f32[4,1,64,32]{2,0,3,1:T(4,128)S(1)}, f32[4,1,64,32]{2,0,3,1:T(4,128)}, u32[]{:S(2)}) copy-start(f32[4,1,64,32]{2,0,3,1:T(4,128)} %reshape.467) | copy-start | bytes 98308
  55.6 10.9 %collective-permute-start.4 = (bf16[4,1,8,8,32]{4,3,2,0,1:T(8,128)(2,1)}, bf16[4,1,8,8,32]{4,3,2,0,1:T(8,128)(2,1)}, u32[]{:S(2)}, u32[]{:S(2)}) collective-permute-start(bf16[4,1,8,8,32]{4,3,2,0,1:T(8,128)(2,1)} %fusion.35), channel_id=1, source_target_pairs={{0,4},{4,8},{8,12},{12,16},{16,20},{20,24},{24,28},{1,5},{5,9},{9,... | collective-permute-start | bytes 49160 | tf_op jit(solution)/shard_map/ppermute | solution.py:18
  61.3 5.9 %collective-permute-start.5 = (bf16[4,1,8,8,32]{4,3,2,0,1:T(8,128)(2,1)}, bf16[4,1,8,8,32]{4,3,2,0,1:T(8,128)(2,1)}, u32[]{:S(2)}, u32[]{:S(2)}) collective-permute-start(bf16[4,1,8,8,32]{4,3,2,0,1:T(8,128)(2,1)} %fusion.35), channel_id=1, source_target_pairs={{4,0},{8,4},{12,8},{16,12},{20,16},{24,20},{28,24},{5,1},{9,5},{13... | collective-permute-start | bytes 49160 | tf_op jit(solution)/shard_map/ppermute | solution.py:19
  82.0 1.2 copy-start.25
  83.4 1.1 copy-start.21
  109.7 1.1 copy-start.1
  141.1 3.0 %copy-start.3 = (f32[4,8,48,128]{3,2,1,0:T(8,128)S(1)}, f32[4,8,48,128]{3,2,1,0:T(8,128)}, u32[]{:S(2)}) copy-start(f32[4,8,48,128]{3,2,1,0:T(8,128)} %get-tuple-element.7) | copy-start | bytes 2359300
  145.2 9.4 %collective-permute-start.6 = (bf16[1,1,16,16,64]{4,3,2,1,0:T(8,128)(2,1)}, bf16[1,1,16,16,64]{4,3,2,1,0:T(8,128)(2,1)S(1)}, u32[]{:S(2)}, u32[]{:S(2)}) collective-permute-start(bf16[1,1,16,16,64]{4,3,2,1,0:T(8,128)(2,1)} %get-tuple-element.127), channel_id=1, source_target_pairs={{0,4},{4,8},{8,12},{12,16},{16,20},{20,24},{24,28},{1,5},{5,9},{9,... | collective-permute-start | bytes 98312 | tf_op jit(solution)/shard_map/ppermute | solution.py:18
  148.6 5.9 %collective-permute-start.7 = (bf16[1,1,16,16,64]{4,3,2,1,0:T(8,128)(2,1)}, bf16[1,1,16,16,64]{4,3,2,1,0:T(8,128)(2,1)}, u32[]{:S(2)}, u32[]{:S(2)}) collective-permute-start(bf16[1,1,16,16,64]{4,3,2,1,0:T(8,128)(2,1)} %get-tuple-element.128), channel_id=1, source_target_pairs={{4,0},{8,4},{12,8},{16,12},{20,16},{24,20},{28,24},{5,1},{9,5},{13... | collective-permute-start | bytes 98312 | tf_op jit(solution)/shard_map/ppermute | solution.py:19
  150.8 1.1 copy-start.2
  (32 other events, 25.9 us)
Sparse Core Ops, SparseCore 0:
  85.5 23.0 reduce-scatter.3

commit v2 on v1

--- a/solution.py
+++ b/solution.py
@@ -96,14 +96,6 @@
     return jnp.transpose(shaped, (0, 1, 4, 2, 5, 3, 6, 7)).reshape(
         samples, extent_z, extent_x, extent_y, channels
     )
-
-
-def coarse_rim(block):
-    return with_halo(block, (("gz", 1),), 1)
-
-
-def coarse_grad_rim(block):
-    return with_halo(block, (("gz", 1),), 1)
 
 
 MESH = pl.DeviceIdType.MESH
@@ -306,11 +298,136 @@
     )
 
 
+def spread_kernel(
+    groups, slabs, shared, src_ref, out_ref, inbox, mid_send, mid_recv, up_send, up_recv, down_send,
+    down_recv,
+):
+    z = lax.axis_index("gz")
+    g = lax.axis_index("grp")
+    planes = src_ref.shape[1]
+
+    def at_grp(step):
+        return lax.rem(g + step, groups)
+
+    def block(step):
+        return 0 if shared else at_grp(step)
+
+    def greet(level, steps):
+        for step in steps:
+            pl.semaphore_signal(
+                barrier, inc=1, device_id=(level, at_grp(step)), device_id_type=MESH
+            )
+
+    def middle(k):
+        return exchange(
+            src_ref.at[block(k)], inbox.at[g, pl.ds(1, planes)], mid_send, mid_recv, k - 1,
+            (z, at_grp(k)),
+        )
+
+    def upward(k):
+        return exchange(
+            src_ref.at[block(k), planes - 1], inbox.at[g, 0], up_send, up_recv, k,
+            (z + 1, at_grp(k)),
+        )
+
+    def downward(k):
+        return exchange(
+            src_ref.at[block(k), 0], inbox.at[g, planes + 1], down_send, down_recv, k,
+            (z - 1, at_grp(k)),
+        )
+
+    barrier = pltpu.get_barrier_semaphore()
+    below = z > 0
+    above = z < slabs - 1
+    greet(z, range(1, groups))
+
+    @pl.when(below)
+    def _():
+        greet(z - 1, range(groups))
+
+    @pl.when(above)
+    def _():
+        greet(z + 1, range(groups))
+
+    sides = below.astype(jnp.int32) + above.astype(jnp.int32)
+    pl.semaphore_wait(barrier, groups - 1 + groups * sides)
+
+    @pl.when(above)
+    def _():
+        for k in range(groups):
+            upward(k).start()
+
+    @pl.when(below)
+    def _():
+        for k in range(groups):
+            downward(k).start()
+
+    for k in range(1, groups):
+        middle(k).start()
+
+    out_ref[g, pl.ds(1, planes)] = src_ref[block(0)]
+    for k in range(1, groups):
+        middle(k).wait()
+        source = lax.rem(g + groups - k, groups)
+        out_ref[source, pl.ds(1, planes)] = inbox[source, pl.ds(1, planes)]
+
+    @pl.when(above)
+    def _():
+        for k in range(groups):
+            upward(k).wait_send()
+            downward(k).wait_recv()
+        out_ref[:, planes + 1] = inbox[:, planes + 1]
+
+    @pl.when(below)
+    def _():
+        for k in range(groups):
+            downward(k).wait_send()
+            upward(k).wait_recv()
+        out_ref[:, 0] = inbox[:, 0]
+
+    @pl.when(jnp.logical_not(above))
+    def _():
+        out_ref[:, planes + 1] = jnp.zeros_like(out_ref[:, planes + 1])
+
+    @pl.when(jnp.logical_not(below))
+    def _():
+        out_ref[:, 0] = jnp.zeros_like(out_ref[:, 0])
+
+
+def spread(blocks, number):
+    slabs, groups = lax.axis_size("gz"), lax.axis_size("grp")
+    shared = blocks.shape[0] == 1
+    planes = blocks.shape[1]
+    shape = (groups, planes + 2) + blocks.shape[2:]
+    vmem = pl.BlockSpec(memory_space=pltpu.VMEM)
+    dma = pltpu.SemaphoreType.DMA
+    return pl.pallas_call(
+        functools.partial(spread_kernel, groups, slabs, shared),
+        out_shape=jax.ShapeDtypeStruct(shape, blocks.dtype),
+        in_specs=[vmem],
+        out_specs=vmem,
+        scratch_shapes=[
+            pltpu.VMEM(shape, blocks.dtype),
+            dma((groups - 1,)),
+            dma((groups - 1,)),
+            dma((groups,)),
+            dma((groups,)),
+            dma((groups,)),
+            dma((groups,)),
+        ],
+        compiler_params=pltpu.CompilerParams(collective_id=number, has_side_effects=True),
+    )(blocks)
+
+
 def per_device(volumes, cotangent, fine_kernel, down_kernel, coarse_kernel):
     samples, planes, xfine, packed = volumes.shape
     cfine = fine_kernel.shape[1]
     yfine = packed // cfine
     fine = volumes.reshape(samples, planes, xfine, yfine, cfine)
+    local = flip_kernel(coarse_kernel, coarse_kernel.shape[0] // 27)
+    flipped = lax.all_gather(
+        local.reshape(27, coarse_kernel.shape[1], -1), "grp", axis=1, tiled=True
+    ).reshape(coarse_kernel.shape[0], -1)
     fine_padded = pad_sides(with_halo(fine, (("gz", 1),), 1))
     fine_pre = convolve(fine_padded, fine_kernel)
     fine_act = jax.nn.silu(fine_pre).astype(jnp.bfloat16)
@@ -319,8 +436,10 @@
         jnp.bfloat16
     )
     coarse_in = coarse_in.reshape(samples, planes // 2, xfine // 2, yfine // 2, -1)
-    coarse_framed = coarse_rim(coarse_in)
-    gathered = pad_sides(lax.all_gather(coarse_framed, "grp", axis=0, tiled=True))
+    planes_c, x_c, y_c, channels_c = coarse_in.shape[1:]
+    gathered = pad_sides(
+        lax.all_gather(with_halo(coarse_in, (("gz", 1),), 1), "grp", axis=0, tiled=True)
+    )
     coarse_pre = convolve(gathered, coarse_kernel)
     group, zcoarse, xcoarse, ycoarse, own_channels = coarse_pre.shape
     coarse_out = (
@@ -331,13 +450,13 @@
     grad_shaped = cotangent.reshape(coarse_pre.shape).astype(jnp.float32)
     coarse_grad = (grad_shaped * silu_slope(coarse_pre)).astype(jnp.bfloat16)
     coarse_kg = kernel_gradient(gathered, coarse_grad)
-    partial_value = convolve(
-        pad_sides(coarse_grad_rim(coarse_grad)),
-        flip_kernel(coarse_kernel, coarse_kernel.shape[0] // 27),
-    )
-    coarse_in_grad = lax.psum_scatter(
-        partial_value.astype(jnp.bfloat16), "grp", scatter_dimension=0, tiled=True
-    )
+    groups = lax.axis_size("grp")
+    to_send = coarse_grad.reshape(groups, samples, planes_c, x_c * y_c, own_channels)
+    arrived = spread(jnp.swapaxes(to_send, 1, 2), 2)
+    own_grad = jnp.transpose(arrived, (2, 1, 3, 0, 4)).reshape(
+        samples, planes_c + 2, x_c, y_c, channels_c
+    )
+    coarse_in_grad = convolve(pad_sides(own_grad), flipped).astype(jnp.bfloat16)
     flat_in_grad = coarse_in_grad.reshape(-1, coarse_in_grad.shape[-1])
     pooled_grad = jnp.dot(flat_in_grad, down_kernel.T, preferred_element_type=jnp.float32)
     fine_act_grad = unpool_columns(pooled_grad, samples, planes, xfine, yfine, cfine)

time: 183 us -> 148 us (0.81)
  waiting for transfers between devices: 21.7 us -> 0.02 us
  between operations: 15 us -> 1.5 us
  blocking collectives: 6.7 us -> 17.9 us
  local copies, waits for them, and re-layouts: 65.5 us -> 54.7 us
  Pallas kernels: 28 us -> 36.4 us
  starting transfers between devices: 25.2 us -> 18.9 us
    unnamed x2 -> x0, waiting for transfers between devices: 21.1 us -> none
    all_gather x1 -> x2, blocking collectives: 6.7 us -> 17.9 us  [the longest x1 11.2 us: per_device(): lax.all_gather(local.reshape(27, coarse_kernel.shape[1], -1), 'grp', axis...]
    pallas_call x0 -> x1, Pallas kernels: none -> 9.48 us  [spread(): pl.pallas_call(functools.partial(spread_kernel, groups, slabs, shared), o...]
    concatenate x30 -> x22, local copies, waits for them, and re-layouts: 20.8 us -> 12.8 us  [convolve(): columns = jnp.concatenate(pieces, axis=-1).reshape(-1, 9 * channels)]
    ppermute x4 -> x3, starting transfers between devices: 17.3 us -> 12.9 us  [with_halo(): before = lax.ppermute(last, axis, up)]
    convert_element_type x4 -> x0, local copies, waits for them, and re-layouts: 2.32 us -> none  [the longest x3 1.47 us: per_device(): grad_shaped = cotangent.reshape(coarse_pre.shape).astype(jnp.float32)]
    unnamed x133 -> x116, local copies, waits for them, and re-layouts: 19.3 us -> 17.1 us
    ppermute x4 -> x3, starting transfers between devices: 7.86 us -> 5.94 us  [with_halo(): after = lax.ppermute(initial, axis, down)]
  transfers between devices with their start and end apart: 9 -> 6, of which waited for: 2 -> 0; matrix products, arithmetic and copies ran while one was open for 10% -> 10% of each run, Pallas kernels for 0% -> 0%
where the time goes in v2:
time: 148 us; the launch traced here: 146 us
  local copies, waits for them, and re-layouts  54.7 us (37%)
  Pallas kernels  36.4 us (25%)
  starting transfers between devices  18.9 us (13%)
  blocking collectives  17.9 us (12%)
  matrix products  10.5 us (7%)
  other arithmetic  6.55 us (4%)
  between operations  1.5 us (1%)
    pallas_call x1, Pallas kernels, kernel_totals(): pl.pallas_call(functools.partial(totals_kernel, groups, slabs), out_shape...  26.9 us
    unnamed x116, local copies, waits for them, and re-layouts  17.1 us
    ppermute x3, starting transfers between devices, with_halo(): before = lax.ppermute(last, axis, up)  12.9 us
    concatenate x22, local copies, waits for them, and re-layouts, convolve(): columns = jnp.concatenate(pieces, axis=-1).reshape(-1, 9 * channels)  12.8 us
    all_gather x1, blocking collectives, per_device(): lax.all_gather(local.reshape(27, coarse_kernel.shape[1], -1), 'grp', axis...  11.2 us
    pallas_call x1, Pallas kernels, spread(): pl.pallas_call(functools.partial(spread_kernel, groups, slabs, shared), o...  9.48 us
    dot_general x12, matrix products, convolve(): partial_value = jnp.dot(columns, rows, preferred_element_type=jnp.float32)  7.67 us
    all_gather x1, blocking collectives, per_device(): lax.all_gather(with_halo(coarse_in, (('gz', 1),), 1), 'grp', axis=0, tile...  6.66 us
  transfers between devices with their start and end apart: 6, of which 0 were waited for; matrix products, arithmetic and copies ran while one was open for 10% of the time, Pallas kernels for 0%

profile of v2, /device:TPU:1, one launch (start us, length us, event | category | flops | bytes accessed | tf_op | source)
XLA Modules:
  0.0 146.4 jit_solution(8738162406264279430)
XLA Ops:
  1.7 4.6 %collective-permute-start = (bf16[1,1,16,16,64]{4,3,2,1,0:T(8,128)(2,1)S(1)}, bf16[1,1,16,16,64]{4,3,2,1,0:T(8,128)(2,1)S(1)}, u32[]{:S(2)}, u32[]{:S(2)}) collective-permute-start(bf16[1,1,16,16,64]{4,3,2,1,0:T(8,128)(2,1)S(1)} %get-tuple-element.94), channel_id=1, source_target_pairs={{0,4},{4,8},{8,12},{12,16},{16,20},{20,24},{24,28},{1,5},{5,9},{9,... | collective-permute-start | bytes 98312 | tf_op jit(solution)/shard_map/ppermute | solution.py:18
  6.3 1.9 %collective-permute-start.1 = (bf16[1,1,16,16,64]{4,3,2,1,0:T(8,128)(2,1)S(1)}, bf16[1,1,16,16,64]{4,3,2,1,0:T(8,128)(2,1)S(1)}, u32[]{:S(2)}, u32[]{:S(2)}) collective-permute-start(bf16[1,1,16,16,64]{4,3,2,1,0:T(8,128)(2,1)S(1)} %get-tuple-element.95), channel_id=1, source_target_pairs={{4,0},{8,4},{12,8},{16,12},{20,16},{24,20},{28,24},{5,1},{9,5},{13... | collective-permute-start | bytes 98312 | tf_op jit(solution)/shard_map/ppermute | solution.py:19
  9.1 11.2 %all_gather.7 = bf16[27,128,128]{2,1,0:T(8,128)(2,1)S(1)} all-gather(bf16[27,32,128]{2,1,0:T(8,128)(2,1)S(1)} %bitcast.211), channel_id=1, replica_groups=mesh['gz'=8,'grp'=4] {'grp'}, dimensions={1}, use_global_device_ids=true | all-gather | bytes 1105920 | tf_op jit(solution)/shard_map/all_gather | solution.py:428
  21.8 1.7 %rev.7 = bf16[3,3,3,64,64]{3,2,1,0,4:T(4,128)(2,1)S(1)} reverse(bf16[3,3,3,64,64]{3,2,1,0,4:T(4,128)(2,1)S(1)} %reshape.479), dimensions={0,1,2} | reverse | bytes 442368 | tf_op jit(solution)/shard_map/rev | solution.py:79
  27.9 1.3 concatenate.134
  29.2 1.9 %convolution_add_fusion.3 = f32[512,64]{0,1:T(8,128)} fusion(f32[512,64]{0,1:T(8,128)} %fusion.37, bf16[512,576]{1,0:T(8,128)(2,1)S(1)} %bitcast.177, bf16[1728,64]{0,1:T(8,128)(2,1)S(1)} %copy-done.9), kind=kOutput, calls=%fused_computation.42 | convolution fusion | flops 37781504 | bytes 999424 | tf_op jit(solution)/shard_map/dot_general | solution.py:46
  31.1 1.5 %concatenate.146 = bf16[1,2,16,16,576]{4,3,2,1,0:T(8,128)(2,1)S(1)} concatenate(bf16[1,2,16,16,64]{4,3,2,1,0:T(8,128)(2,1)} %get-tuple-element.62, bf16[1,2,16,16,64]{4,3,2,1,0:T(8,128)(2,1)} %get-tuple-element.61, bf16[1,2,16,16,64]{4,3,2,1,0:T(8,128)(2,1)} %get-tuple-element.60, bf16[1,2,16,16,64]{4,3,2,1,0:T(8,128)(2,1)} %get-tuple-element.59, ...), dimensions={4} | concatenate | bytes 1179648 | tf_op jit(solution)/shard_map/concatenate | solution.py:44
  32.7 1.9 %convolution_add_fusion.2 = f32[512,64]{0,1:T(8,128)} fusion(f32[512,64]{0,1:T(8,128)S(1)} %copy-done.19, bf16[512,576]{1,0:T(8,128)(2,1)S(1)} %bitcast.178, bf16[1728,64]{0,1:T(8,128)(2,1)} %param.7), kind=kOutput, calls=%fused_computation.41 | convolution fusion | flops 37781504 | bytes 933888 | tf_op jit(solution)/shard_map/dot_general | solution.py:46
  37.6 4.9 %collective-permute-start.2 = (bf16[1,1,8,8,128]{4,3,2,0,1:T(8,128)(2,1)S(1)}, bf16[1,1,8,8,128]{4,3,2,0,1:T(8,128)(2,1)}, u32[]{:S(2)}, u32[]{:S(2)}) collective-permute-start(bf16[1,1,8,8,128]{4,3,2,0,1:T(8,128)(2,1)S(1)} %fusion.8), channel_id=1, source_target_pairs={{0,4},{4,8},{8,12},{12,16},{16,20},{20,24},{24,28},{1,5},{5,9},{9,... | collective-permute-start | bytes 49160 | tf_op jit(solution)/shard_map/ppermute | solution.py:18
  42.5 1.9 %collective-permute-start.3 = (bf16[1,1,8,8,128]{4,3,2,0,1:T(8,128)(2,1)S(1)}, bf16[1,1,8,8,128]{4,3,2,0,1:T(8,128)(2,1)}, u32[]{:S(2)}, u32[]{:S(2)}) collective-permute-start(bf16[1,1,8,8,128]{4,3,2,0,1:T(8,128)(2,1)S(1)} %fusion.8), channel_id=1, source_target_pairs={{4,0},{8,4},{12,8},{16,12},{20,16},{24,20},{28,24},{5,1},{9,5},{13... | collective-permute-start | bytes 49160 | tf_op jit(solution)/shard_map/ppermute | solution.py:19
  45.4 1.5 %copy.37 = bf16[4,1,64,32]{3,2,0,1:T(8,128)(2,1)} copy(bf16[4,1,64,32]{2,3,1,0:T(8,128)(2,1)} %param.6) | data formatting | bytes 32768 | tf_op args[1]
  46.9 1.6 %copy.54 = bf16[1,3,3,64,64]{4,3,2,1,0:T(8,128)(2,1)} copy(bf16[1,3,3,64,64]{4,2,1,0,3:T(4,128)(2,1)} %get-tuple-element.25) | data formatting | bytes 147456 | tf_op jit(solution)/shard_map/slice | solution.py:45
  52.1 6.7 %all_gather.6 = bf16[4,3,8,8,128]{4,3,2,0,1:T(8,128)(2,1)S(1)} all-gather(bf16[1,3,8,8,128]{4,3,2,0,1:T(8,128)(2,1)S(1)} %pad_maximum_fusion.8), channel_id=1, replica_groups=mesh['gz'=8,'grp'=4] {'grp'}, dimensions={0}, use_global_device_ids=true | all-gather | bytes 245760 | tf_op jit(solution)/shard_map/all_gather | solution.py:441
  62.0 1.5 %copy.36 = f32[256,32]{1,0:T(8,128)} copy(f32[256,32]{0,1:T(8,128)} %convolution_add_fusion.4) | data formatting | bytes 65536 | tf_op jit(solution)/shard_map/add | solution.py:47
  63.5 1.6 %fusion.34 = (bf16[4,1,64,32]{3,2,0,1:T(8,128)(2,1)S(1)}, bf16[4,1,64,32]{3,2,0,1:T(8,128)(2,1)}) fusion(bf16[4,1,64,32]{3,2,0,1:T(8,128)(2,1)} %copy.37, f32[4,1,64,32]{3,2,0,1:T(8,128)} %bitcast.207), kind=kLoop, calls=%fused_computation.119 | loop fusion | flops 98304 | bytes 81920 | tf_op jit(solution)/shard_map/convert_element_type | solution.py:451
  67.9 9.5 %shard_map.92 = bf16[4,3,1,64,32]{4,3,2,1,0:T(8,128)(2,1)} custom-call(bf16[4,1,1,64,32]{4,3,2,1,0:T(8,128)(2,1)} %fusion.33.src_ref), custom_call_target="tpu_custom_call" | custom-call | tf_op jit(solution)/shard_map/pallas_call | solution.py:404
  85.7 26.9 %shard_map.93 = (f32[4,8,48,128]{3,2,1,0:T(8,128)}, f32[8,112,128]{2,1,0:T(8,128)}) custom-call(bf16[4,8,48,128]{3,2,1,0:T(8,128)(2,1)} %bitcast.195, bf16[8,112,128]{2,1,0:T(8,128)(2,1)} %bitcast.210), custom_call_target="tpu_custom_call" | custom-call | tf_op jit(solution)/shard_map/pallas_call | solution.py:269
  112.6 2.8 %fusion.51 = (f32[864,32]{1,0:T(8,128)S(1)}, f32[864,32]{1,0:T(8,128)S(1)}, f32[864,32]{1,0:T(8,128)}, f32[864,32]{1,0:T(8,128)S(1)}) fusion(f32[896,128]{1,0:T(8,128)} %bitcast.176), kind=kLoop, calls=%fused_computation.207 | loop fusion | bytes 884736 | tf_op jit(solution)/shard_map/slice | solution.py:246
  116.5 3.4 %collective-permute-start.4 = (bf16[1,1,16,16,64]{4,3,2,1,0:T(8,128)(2,1)}, bf16[1,1,16,16,64]{4,3,2,1,0:T(8,128)(2,1)S(1)}, u32[]{:S(2)}, u32[]{:S(2)}) collective-permute-start(bf16[1,1,16,16,64]{4,3,2,1,0:T(8,128)(2,1)} %get-tuple-element.90), channel_id=1, source_target_pairs={{0,4},{4,8},{8,12},{12,16},{16,20},{20,24},{24,28},{1,5},{5,9},{9,... | collective-permute-start | bytes 98312 | tf_op jit(solution)/shard_map/ppermute | solution.py:18
  119.9 2.1 %collective-permute-start.5 = (bf16[1,1,16,16,64]{4,3,2,1,0:T(8,128)(2,1)}, bf16[1,1,16,16,64]{4,3,2,1,0:T(8,128)(2,1)}, u32[]{:S(2)}, u32[]{:S(2)}) collective-permute-start(bf16[1,1,16,16,64]{4,3,2,1,0:T(8,128)(2,1)} %get-tuple-element.91), channel_id=1, source_target_pairs={{4,0},{8,4},{12,8},{16,12},{20,16},{24,20},{28,24},{5,1},{9,5},{13... | collective-permute-start | bytes 98312 | tf_op jit(solution)/shard_map/ppermute | solution.py:19
  130.3 1.6 %copy.47 = bf16[512,64]{0,1:T(8,128)(2,1)} copy(bf16[512,64]{1,0:T(8,128)(2,1)} %bitcast.222) | data formatting | bytes 131072 | tf_op jit(solution)/shard_map/concatenate | solution.py:44
  131.9 1.6 %copy.48 = bf16[512,64]{0,1:T(8,128)(2,1)} copy(bf16[512,64]{1,0:T(8,128)(2,1)} %bitcast.221) | data formatting | bytes 131072 | tf_op jit(solution)/shard_map/concatenate | solution.py:44
  133.5 1.6 %copy.49 = bf16[512,64]{0,1:T(8,128)(2,1)} copy(bf16[512,64]{1,0:T(8,128)(2,1)} %bitcast.220) | data formatting | bytes 131072 | tf_op jit(solution)/shard_map/concatenate | solution.py:44
  135.1 1.6 %copy.50 = bf16[512,64]{0,1:T(8,128)(2,1)} copy(bf16[512,64]{1,0:T(8,128)(2,1)} %bitcast.219) | data formatting | bytes 131072 | tf_op jit(solution)/shard_map/concatenate | solution.py:44
  (200 shorter events, 47.9 us)
Async XLA Ops:
  0.6 36.8 %copy-start = (bf16[512,128]{1,0:T(8,128)(2,1)S(1)}, bf16[512,128]{1,0:T(8,128)(2,1)}, u32[]{:S(2)}) copy-start(bf16[512,128]{1,0:T(8,128)(2,1)} %param.8) | copy-start | bytes 393220
  0.6 7.6 %copy-start.10 = (bf16[3456,32]{0,1:T(8,128)(2,1)S(1)}, bf16[3456,32]{0,1:T(8,128)(2,1)}, u32[]{:S(2)}) copy-start(bf16[3456,32]{0,1:T(8,128)(2,1)} %param.9) | copy-start | bytes 663556
  1.7 21.8 %collective-permute-start = (bf16[1,1,16,16,64]{4,3,2,1,0:T(8,128)(2,1)S(1)}, bf16[1,1,16,16,64]{4,3,2,1,0:T(8,128)(2,1)S(1)}, u32[]{:S(2)}, u32[]{:S(2)}) collective-permute-start(bf16[1,1,16,16,64]{4,3,2,1,0:T(8,128)(2,1)S(1)} %get-tuple-element.94), channel_id=1, source_target_pairs={{0,4},{4,8},{8,12},{12,16},{16,20},{20,24},{24,28},{1,5},{5,9},{9,... | collective-permute-start | bytes 98312 | tf_op jit(solution)/shard_map/ppermute | solution.py:18
  6.3 17.2 %collective-permute-start.1 = (bf16[1,1,16,16,64]{4,3,2,1,0:T(8,128)(2,1)S(1)}, bf16[1,1,16,16,64]{4,3,2,1,0:T(8,128)(2,1)S(1)}, u32[]{:S(2)}, u32[]{:S(2)}) collective-permute-start(bf16[1,1,16,16,64]{4,3,2,1,0:T(8,128)(2,1)S(1)} %get-tuple-element.95), channel_id=1, source_target_pairs={{4,0},{8,4},{12,8},{16,12},{20,16},{24,20},{28,24},{5,1},{9,5},{13... | collective-permute-start | bytes 98312 | tf_op jit(solution)/shard_map/ppermute | solution.py:19
  20.3 0.9 copy-start.20
  20.3 1.2 copy-start.9
  26.1 1.0 copy-start.27
  31.1 1.6 %copy-start.19 = (f32[512,64]{0,1:T(8,128)S(1)}, f32[512,64]{0,1:T(8,128)}, u32[]{:S(2)}) copy-start(f32[512,64]{0,1:T(8,128)} %convolution_add_fusion.3) | copy-start | bytes 393220
  37.6 13.8 %collective-permute-start.2 = (bf16[1,1,8,8,128]{4,3,2,0,1:T(8,128)(2,1)S(1)}, bf16[1,1,8,8,128]{4,3,2,0,1:T(8,128)(2,1)}, u32[]{:S(2)}, u32[]{:S(2)}) collective-permute-start(bf16[1,1,8,8,128]{4,3,2,0,1:T(8,128)(2,1)S(1)} %fusion.8), channel_id=1, source_target_pairs={{0,4},{4,8},{8,12},{12,16},{16,20},{20,24},{24,28},{1,5},{5,9},{9,... | collective-permute-start | bytes 49160 | tf_op jit(solution)/shard_map/ppermute | solution.py:18
  42.5 8.9 %collective-permute-start.3 = (bf16[1,1,8,8,128]{4,3,2,0,1:T(8,128)(2,1)S(1)}, bf16[1,1,8,8,128]{4,3,2,0,1:T(8,128)(2,1)}, u32[]{:S(2)}, u32[]{:S(2)}) collective-permute-start(bf16[1,1,8,8,128]{4,3,2,0,1:T(8,128)(2,1)S(1)} %fusion.8), channel_id=1, source_target_pairs={{4,0},{8,4},{12,8},{16,12},{20,16},{24,20},{28,24},{5,1},{9,5},{13... | collective-permute-start | bytes 49160 | tf_op jit(solution)/shard_map/ppermute | solution.py:19
  46.9 1.6 %copy-start.13 = (bf16[1,3,3,64,64]{4,2,1,0,3:T(4,128)(2,1)S(1)}, bf16[1,3,3,64,64]{4,2,1,0,3:T(4,128)(2,1)}, u32[]{:S(2)}) copy-start(bf16[1,3,3,64,64]{4,2,1,0,3:T(4,128)(2,1)} %get-tuple-element.26) | copy-start | bytes 221188
  48.5 1.0 copy-start.12
  59.6 0.9 copy-start.11
  66.3 0.9 copy-start.8
  66.3 0.9 copy-start.14
  78.9 1.0 copy-start.7
  79.1 1.0 copy-start.6
  80.1 1.0 copy-start.5
  82.4 1.1 copy-start.1
  112.6 2.8 %copy-start.3 = (f32[4,8,48,128]{3,2,1,0:T(8,128)S(1)}, f32[4,8,48,128]{3,2,1,0:T(8,128)}, u32[]{:S(2)}) copy-start(f32[4,8,48,128]{3,2,1,0:T(8,128)} %get-tuple-element.7) | copy-start | bytes 2359300
  116.5 10.8 %collective-permute-start.4 = (bf16[1,1,16,16,64]{4,3,2,1,0:T(8,128)(2,1)}, bf16[1,1,16,16,64]{4,3,2,1,0:T(8,128)(2,1)S(1)}, u32[]{:S(2)}, u32[]{:S(2)}) collective-permute-start(bf16[1,1,16,16,64]{4,3,2,1,0:T(8,128)(2,1)} %get-tuple-element.90), channel_id=1, source_target_pairs={{0,4},{4,8},{8,12},{12,16},{16,20},{20,24},{24,28},{1,5},{5,9},{9,... | collective-permute-start | bytes 98312 | tf_op jit(solution)/shard_map/ppermute | solution.py:18
  119.9 7.3 %collective-permute-start.5 = (bf16[1,1,16,16,64]{4,3,2,1,0:T(8,128)(2,1)}, bf16[1,1,16,16,64]{4,3,2,1,0:T(8,128)(2,1)}, u32[]{:S(2)}, u32[]{:S(2)}) collective-permute-start(bf16[1,1,16,16,64]{4,3,2,1,0:T(8,128)(2,1)} %get-tuple-element.91), channel_id=1, source_target_pairs={{4,0},{8,4},{12,8},{16,12},{20,16},{24,20},{28,24},{5,1},{9,5},{13... | collective-permute-start | bytes 98312 | tf_op jit(solution)/shard_map/ppermute | solution.py:19
  122.1 1.1 copy-start.2
  138.6 0.9 copy-start.4
  (13 other events, 10.8 us)

commit v3 on v2

--- a/solution.py
+++ b/solution.py
@@ -320,19 +320,19 @@
 
     def middle(k):
         return exchange(
-            src_ref.at[block(k)], inbox.at[g, pl.ds(1, planes)], mid_send, mid_recv, k - 1,
+            src_ref.at[block(k)], inbox.at[k, pl.ds(1, planes)], mid_send, mid_recv, k - 1,
             (z, at_grp(k)),
         )
 
     def upward(k):
         return exchange(
-            src_ref.at[block(k), planes - 1], inbox.at[g, 0], up_send, up_recv, k,
+            src_ref.at[block(k), planes - 1], inbox.at[k, 0], up_send, up_recv, k,
             (z + 1, at_grp(k)),
         )
 
     def downward(k):
         return exchange(
-            src_ref.at[block(k), 0], inbox.at[g, planes + 1], down_send, down_recv, k,
+            src_ref.at[block(k), 0], inbox.at[k, planes + 1], down_send, down_recv, k,
             (z - 1, at_grp(k)),
         )
 
@@ -365,11 +365,10 @@
     for k in range(1, groups):
         middle(k).start()
 
-    out_ref[g, pl.ds(1, planes)] = src_ref[block(0)]
+    out_ref[0, pl.ds(1, planes)] = src_ref[block(0)]
     for k in range(1, groups):
         middle(k).wait()
-        source = lax.rem(g + groups - k, groups)
-        out_ref[source, pl.ds(1, planes)] = inbox[source, pl.ds(1, planes)]
+        out_ref[k, pl.ds(1, planes)] = inbox[k, pl.ds(1, planes)]
 
     @pl.when(above)
     def _():
@@ -424,11 +423,13 @@
     cfine = fine_kernel.shape[1]
     yfine = packed // cfine
     fine = volumes.reshape(samples, planes, xfine, yfine, cfine)
+    fine_padded = pad_sides(with_halo(fine, (("gz", 1),), 1))
     local = flip_kernel(coarse_kernel, coarse_kernel.shape[0] // 27)
-    flipped = lax.all_gather(
-        local.reshape(27, coarse_kernel.shape[1], -1), "grp", axis=1, tiled=True
-    ).reshape(coarse_kernel.shape[0], -1)
-    fine_padded = pad_sides(with_halo(fine, (("gz", 1),), 1))
+    groups = lax.axis_size("grp")
+    kernel_parts = [local] + [
+        lax.ppermute(local, "grp", [(i, (i + step) % groups) for i in range(groups)])
+        for step in range(1, groups)
+    ]
     fine_pre = convolve(fine_padded, fine_kernel)
     fine_act = jax.nn.silu(fine_pre).astype(jnp.bfloat16)
     pooled = pool_columns(fine_act)
@@ -450,12 +451,14 @@
     grad_shaped = cotangent.reshape(coarse_pre.shape).astype(jnp.float32)
     coarse_grad = (grad_shaped * silu_slope(coarse_pre)).astype(jnp.bfloat16)
     coarse_kg = kernel_gradient(gathered, coarse_grad)
-    groups = lax.axis_size("grp")
     to_send = coarse_grad.reshape(groups, samples, planes_c, x_c * y_c, own_channels)
     arrived = spread(jnp.swapaxes(to_send, 1, 2), 2)
     own_grad = jnp.transpose(arrived, (2, 1, 3, 0, 4)).reshape(
         samples, planes_c + 2, x_c, y_c, channels_c
     )
+    flipped = jnp.concatenate(
+        [part.reshape(27, own_channels, channels_c) for part in kernel_parts], axis=1
+    ).reshape(-1, channels_c)
     coarse_in_grad = convolve(pad_sides(own_grad), flipped).astype(jnp.bfloat16)
     flat_in_grad = coarse_in_grad.reshape(-1, coarse_in_grad.shape[-1])
     pooled_grad = jnp.dot(flat_in_grad, down_kernel.T, preferred_element_type=jnp.float32)

time: 148 us -> 140 us (0.946)
  blocking collectives: 17.9 us -> 5.76 us
  starting transfers between devices: 18.9 us -> 22.2 us
    all_gather x1 -> x0, blocking collectives: 11.2 us -> none  [per_device(): lax.all_gather(local.reshape(27, coarse_kernel.shape[1], -1), 'grp', axis...]
    unnamed x116 -> x100, local copies, waits for them, and re-layouts: 17.1 us -> 12.7 us
    ppermute x0 -> x3, starting transfers between devices: none -> 3.6 us  [per_device(): lax.ppermute(local, 'grp', [(i, (i + step) % groups) for i in range(group...]
    concatenate x22, local copies, waits for them, and re-layouts: 12.8 us -> 15 us  [convolve(): columns = jnp.concatenate(pieces, axis=-1).reshape(-1, 9 * channels)]
  transfers between devices with their start and end apart: 6 -> 9, of which waited for: 0 -> 0; matrix products, arithmetic and copies ran while one was open for 10% -> 29% of each run, Pallas kernels for 0% -> 7%
where the time goes in v3:
time: 140 us; the launch traced here: 139 us
  local copies, waits for them, and re-layouts  54.3 us (39%)
  Pallas kernels  37 us (26%)
  starting transfers between devices  22.2 us (16%)
  matrix products  9.86 us (7%)
  other arithmetic  7.91 us (6%)
  blocking collectives  5.76 us (4%)
  between operations  1.52 us (1%)
    pallas_call x1, Pallas kernels, kernel_totals(): pl.pallas_call(functools.partial(totals_kernel, groups, slabs), out_shape...  27.2 us
    concatenate x22, local copies, waits for them, and re-layouts, convolve(): columns = jnp.concatenate(pieces, axis=-1).reshape(-1, 9 * channels)  15 us
    unnamed x100, local copies, waits for them, and re-layouts  12.7 us
    ppermute x3, starting transfers between devices, with_halo(): before = lax.ppermute(last, axis, up)  12.5 us
    pallas_call x1, Pallas kernels, spread(): pl.pallas_call(functools.partial(spread_kernel, groups, slabs, shared), o...  9.8 us
    dot_general x12, matrix products, convolve(): partial_value = jnp.dot(columns, rows, preferred_element_type=jnp.float32)  7.69 us
    ppermute x3, starting transfers between devices, with_halo(): after = lax.ppermute(initial, axis, down)  6.08 us
    all_gather x1, blocking collectives, per_device(): lax.all_gather(with_halo(coarse_in, (('gz', 1),), 1), 'grp', axis=0, tile...  5.76 us
  transfers between devices with their start and end apart: 9, of which 0 were waited for; matrix products, arithmetic and copies ran while one was open for 29% of the time, Pallas kernels for 7%

profile of v3, /device:TPU:1, one launch (start us, length us, event | category | flops | bytes accessed | tf_op | source)
XLA Modules:
  0.0 138.6 jit_solution(12815680829427441977)
XLA Ops:
  1.7 4.6 %collective-permute-start = (bf16[1,1,16,16,64]{4,3,2,1,0:T(8,128)(2,1)S(1)}, bf16[1,1,16,16,64]{4,3,2,1,0:T(8,128)(2,1)S(1)}, u32[]{:S(2)}, u32[]{:S(2)}) collective-permute-start(bf16[1,1,16,16,64]{4,3,2,1,0:T(8,128)(2,1)S(1)} %get-tuple-element.94), channel_id=1, source_target_pairs={{0,4},{4,8},{8,12},{12,16},{16,20},{20,24},{24,28},{1,5},{5,9},{9,... | collective-permute-start | bytes 98312 | tf_op jit(solution)/shard_map/ppermute | solution.py:18
  6.3 2.1 %collective-permute-start.1 = (bf16[1,1,16,16,64]{4,3,2,1,0:T(8,128)(2,1)S(1)}, bf16[1,1,16,16,64]{4,3,2,1,0:T(8,128)(2,1)S(1)}, u32[]{:S(2)}, u32[]{:S(2)}) collective-permute-start(bf16[1,1,16,16,64]{4,3,2,1,0:T(8,128)(2,1)S(1)} %get-tuple-element.95), channel_id=1, source_target_pairs={{4,0},{8,4},{12,8},{16,12},{20,16},{24,20},{28,24},{5,1},{9,5},{13... | collective-permute-start | bytes 98312 | tf_op jit(solution)/shard_map/ppermute | solution.py:19
  14.9 1.7 %rev.7 = bf16[3,3,3,64,64]{3,2,1,0,4:T(4,128)(2,1)S(1)} reverse(bf16[3,3,3,64,64]{3,2,1,0,4:T(4,128)(2,1)S(1)} %reshape.495), dimensions={0,1,2} | reverse | bytes 442368 | tf_op jit(solution)/shard_map/rev | solution.py:79
  22.3 1.9 %convolution_add_fusion.3 = f32[512,64]{0,1:T(8,128)} fusion(f32[512,64]{0,1:T(8,128)} %fusion.37, bf16[512,576]{1,0:T(8,128)(2,1)S(1)} %bitcast.181, bf16[1728,64]{0,1:T(8,128)(2,1)S(1)} %copy-done.6), kind=kOutput, calls=%fused_computation.42 | convolution fusion | flops 37781504 | bytes 999424 | tf_op jit(solution)/shard_map/dot_general | solution.py:46
  24.2 1.5 %concatenate.149 = bf16[1,2,16,16,576]{4,3,2,1,0:T(8,128)(2,1)S(1)} concatenate(bf16[1,2,16,16,64]{4,3,2,1,0:T(8,128)(2,1)} %get-tuple-element.62, bf16[1,2,16,16,64]{4,3,2,1,0:T(8,128)(2,1)} %get-tuple-element.61, bf16[1,2,16,16,64]{4,3,2,1,0:T(8,128)(2,1)} %get-tuple-element.60, bf16[1,2,16,16,64]{4,3,2,1,0:T(8,128)(2,1)} %get-tuple-element.59, ...), dimensions={4} | concatenate | bytes 1179648 | tf_op jit(solution)/shard_map/concatenate | solution.py:44
  25.8 1.9 %convolution_add_fusion.2 = f32[512,64]{0,1:T(8,128)} fusion(f32[512,64]{0,1:T(8,128)S(1)} %copy-done.13, bf16[512,576]{1,0:T(8,128)(2,1)S(1)} %bitcast.182, bf16[1728,64]{0,1:T(8,128)(2,1)} %param.7), kind=kOutput, calls=%fused_computation.41 | convolution fusion | flops 37781504 | bytes 933888 | tf_op jit(solution)/shard_map/dot_general | solution.py:46
  30.7 4.5 %collective-permute-start.2 = (bf16[1,1,8,8,128]{4,3,2,0,1:T(8,128)(2,1)S(1)}, bf16[1,1,8,8,128]{4,3,2,0,1:T(8,128)(2,1)}, u32[]{:S(2)}, u32[]{:S(2)}) collective-permute-start(bf16[1,1,8,8,128]{4,3,2,0,1:T(8,128)(2,1)S(1)} %fusion.8), channel_id=1, source_target_pairs={{0,4},{4,8},{8,12},{12,16},{16,20},{20,24},{24,28},{1,5},{5,9},{9,... | collective-permute-start | bytes 49160 | tf_op jit(solution)/shard_map/ppermute | solution.py:18
  35.2 1.9 %collective-permute-start.3 = (bf16[1,1,8,8,128]{4,3,2,0,1:T(8,128)(2,1)S(1)}, bf16[1,1,8,8,128]{4,3,2,0,1:T(8,128)(2,1)}, u32[]{:S(2)}, u32[]{:S(2)}) collective-permute-start(bf16[1,1,8,8,128]{4,3,2,0,1:T(8,128)(2,1)S(1)} %fusion.8), channel_id=1, source_target_pairs={{4,0},{8,4},{12,8},{16,12},{20,16},{24,20},{28,24},{5,1},{9,5},{13... | collective-permute-start | bytes 49160 | tf_op jit(solution)/shard_map/ppermute | solution.py:19
  38.1 1.5 %copy.37 = bf16[4,1,64,32]{3,2,0,1:T(8,128)(2,1)} copy(bf16[4,1,64,32]{2,3,1,0:T(8,128)(2,1)} %param.6) | data formatting | bytes 32768 | tf_op args[1]
  39.6 1.6 %copy.55 = bf16[1,3,3,64,64]{4,3,2,1,0:T(8,128)(2,1)} copy(bf16[1,3,3,64,64]{4,2,1,0,3:T(4,128)(2,1)} %get-tuple-element.25) | data formatting | bytes 147456 | tf_op jit(solution)/shard_map/slice | solution.py:45
  41.2 1.6 %copy.44 = bf16[1,3,3,64,64]{4,3,2,1,0:T(8,128)(2,1)} copy(bf16[1,3,3,64,64]{4,2,1,0,3:T(4,128)(2,1)} %get-tuple-element.26) | data formatting | bytes 147456 | tf_op jit(solution)/shard_map/slice | solution.py:45
  45.5 5.8 %all_gather.3 = bf16[4,3,8,8,128]{4,3,2,0,1:T(8,128)(2,1)S(1)} all-gather(bf16[1,3,8,8,128]{4,3,2,0,1:T(8,128)(2,1)S(1)} %pad_maximum_fusion.9), channel_id=1, replica_groups=mesh['gz'=8,'grp'=4] {'grp'}, dimensions={0}, use_global_device_ids=true | all-gather | bytes 245760 | tf_op jit(solution)/shard_map/all_gather | solution.py:442
  54.2 1.5 %copy.36 = f32[256,32]{1,0:T(8,128)} copy(f32[256,32]{0,1:T(8,128)} %convolution_add_fusion.4) | data formatting | bytes 65536 | tf_op jit(solution)/shard_map/add | solution.py:47
  55.8 1.6 %fusion.34 = (bf16[4,1,64,32]{3,2,0,1:T(8,128)(2,1)S(1)}, bf16[4,1,64,32]{3,2,0,1:T(8,128)(2,1)}) fusion(bf16[4,1,64,32]{3,2,0,1:T(8,128)(2,1)} %copy.37, f32[4,1,64,32]{3,2,0,1:T(8,128)} %bitcast.211), kind=kLoop, calls=%fused_computation.120 | loop fusion | flops 98304 | bytes 81920 | tf_op jit(solution)/shard_map/convert_element_type | solution.py:452
  59.5 9.8 %shard_map.92 = bf16[4,3,1,64,32]{4,3,2,1,0:T(8,128)(2,1)} custom-call(bf16[4,1,1,64,32]{4,3,2,1,0:T(8,128)(2,1)} %fusion.33.src_ref), custom_call_target="tpu_custom_call" | custom-call | tf_op jit(solution)/shard_map/pallas_call | solution.py:403
  77.9 27.2 %shard_map.93 = (f32[4,8,48,128]{3,2,1,0:T(8,128)}, f32[8,112,128]{2,1,0:T(8,128)}) custom-call(bf16[4,8,48,128]{3,2,1,0:T(8,128)(2,1)} %bitcast.199, bf16[8,112,128]{2,1,0:T(8,128)(2,1)} %bitcast.214), custom_call_target="tpu_custom_call" | custom-call | tf_op jit(solution)/shard_map/pallas_call | solution.py:269
  105.1 2.9 %fusion.51 = (f32[864,32]{1,0:T(8,128)S(1)}, f32[864,32]{1,0:T(8,128)S(1)}, f32[864,32]{1,0:T(8,128)}, f32[864,32]{1,0:T(8,128)S(1)}) fusion(f32[896,128]{1,0:T(8,128)} %bitcast.180), kind=kLoop, calls=%fused_computation.208 | loop fusion | bytes 884736 | tf_op jit(solution)/shard_map/slice | solution.py:246
  109.1 3.4 %collective-permute-start.7 = (bf16[1,1,16,16,64]{4,3,2,1,0:T(8,128)(2,1)}, bf16[1,1,16,16,64]{4,3,2,1,0:T(8,128)(2,1)S(1)}, u32[]{:S(2)}, u32[]{:S(2)}) collective-permute-start(bf16[1,1,16,16,64]{4,3,2,1,0:T(8,128)(2,1)} %get-tuple-element.90), channel_id=1, source_target_pairs={{0,4},{4,8},{8,12},{12,16},{16,20},{20,24},{24,28},{1,5},{5,9},{9,... | collective-permute-start | bytes 98312 | tf_op jit(solution)/shard_map/ppermute | solution.py:18
  112.5 2.1 %collective-permute-start.8 = (bf16[1,1,16,16,64]{4,3,2,1,0:T(8,128)(2,1)}, bf16[1,1,16,16,64]{4,3,2,1,0:T(8,128)(2,1)}, u32[]{:S(2)}, u32[]{:S(2)}) collective-permute-start(bf16[1,1,16,16,64]{4,3,2,1,0:T(8,128)(2,1)} %get-tuple-element.91), channel_id=1, source_target_pairs={{4,0},{8,4},{12,8},{16,12},{20,16},{24,20},{28,24},{5,1},{9,5},{13... | collective-permute-start | bytes 98312 | tf_op jit(solution)/shard_map/ppermute | solution.py:19
  121.5 1.7 %copy.48 = bf16[512,64]{0,1:T(8,128)(2,1)} copy(bf16[512,64]{1,0:T(8,128)(2,1)} %bitcast.225) | data formatting | bytes 131072 | tf_op jit(solution)/shard_map/concatenate | solution.py:44
  123.1 1.6 %copy.49 = bf16[512,64]{0,1:T(8,128)(2,1)} copy(bf16[512,64]{1,0:T(8,128)(2,1)} %bitcast.224) | data formatting | bytes 131072 | tf_op jit(solution)/shard_map/concatenate | solution.py:44
  124.7 1.6 %copy.50 = bf16[512,64]{0,1:T(8,128)(2,1)} copy(bf16[512,64]{1,0:T(8,128)(2,1)} %bitcast.223) | data formatting | bytes 131072 | tf_op jit(solution)/shard_map/concatenate | solution.py:44
  127.1 1.6 %copy.52 = bf16[512,64]{0,1:T(8,128)(2,1)} copy(bf16[512,64]{1,0:T(8,128)(2,1)} %bitcast.221) | data formatting | bytes 131072 | tf_op jit(solution)/shard_map/concatenate | solution.py:44
  128.7 1.6 %copy.53 = bf16[512,64]{0,1:T(8,128)(2,1)} copy(bf16[512,64]{1,0:T(8,128)(2,1)} %bitcast.220) | data formatting | bytes 131072 | tf_op jit(solution)/shard_map/concatenate | solution.py:44
  (189 shorter events, 49.8 us)
Async XLA Ops:
  0.6 29.9 %copy-start = (bf16[512,128]{1,0:T(8,128)(2,1)S(1)}, bf16[512,128]{1,0:T(8,128)(2,1)}, u32[]{:S(2)}) copy-start(bf16[512,128]{1,0:T(8,128)(2,1)} %param.8) | copy-start | bytes 393220
  1.7 12.7 %copy-start.14 = (bf16[1,2,16,1024]{3,2,1,0:T(8,128)(2,1)S(1)}, bf16[1,2,16,1024]{3,2,1,0:T(8,128)(2,1)}, u32[]{:S(2)}) copy-start(bf16[1,2,16,1024]{3,2,1,0:T(8,128)(2,1)} %param.5) | copy-start | bytes 196612
  1.7 14.9 %collective-permute-start = (bf16[1,1,16,16,64]{4,3,2,1,0:T(8,128)(2,1)S(1)}, bf16[1,1,16,16,64]{4,3,2,1,0:T(8,128)(2,1)S(1)}, u32[]{:S(2)}, u32[]{:S(2)}) collective-permute-start(bf16[1,1,16,16,64]{4,3,2,1,0:T(8,128)(2,1)S(1)} %get-tuple-element.94), channel_id=1, source_target_pairs={{0,4},{4,8},{8,12},{12,16},{16,20},{20,24},{24,28},{1,5},{5,9},{9,... | collective-permute-start | bytes 98312 | tf_op jit(solution)/shard_map/ppermute | solution.py:18
  6.3 8.2 %copy-start.6 = (bf16[1728,64]{0,1:T(8,128)(2,1)S(1)}, bf16[1728,64]{0,1:T(8,128)(2,1)}, u32[]{:S(2)}) copy-start(bf16[1728,64]{0,1:T(8,128)(2,1)} %param.7) | copy-start | bytes 663556
  6.3 10.3 %collective-permute-start.1 = (bf16[1,1,16,16,64]{4,3,2,1,0:T(8,128)(2,1)S(1)}, bf16[1,1,16,16,64]{4,3,2,1,0:T(8,128)(2,1)S(1)}, u32[]{:S(2)}, u32[]{:S(2)}) collective-permute-start(bf16[1,1,16,16,64]{4,3,2,1,0:T(8,128)(2,1)S(1)} %get-tuple-element.95), channel_id=1, source_target_pairs={{4,0},{8,4},{12,8},{16,12},{20,16},{24,20},{28,24},{5,1},{9,5},{13... | collective-permute-start | bytes 98312 | tf_op jit(solution)/shard_map/ppermute | solution.py:19
  10.8 61.9 %collective-permute-start.4 = (bf16[864,128]{1,0:T(8,128)(2,1)}, bf16[864,128]{1,0:T(8,128)(2,1)}, u32[]{:S(2)}, u32[]{:S(2)}) collective-permute-start(bf16[864,128]{1,0:T(8,128)(2,1)} %bitcast.26), channel_id=1, source_target_pairs={{0,1},{1,2},{2,3},{3,0},{4,5},{5,6},{6,7},{7,4},{8,9},{9,10},{10,1... | collective-permute-start | bytes 663560 | tf_op jit(solution)/shard_map/ppermute | solution.py:430
  12.0 60.7 %collective-permute-start.5 = (bf16[864,128]{1,0:T(8,128)(2,1)}, bf16[864,128]{1,0:T(8,128)(2,1)}, u32[]{:S(2)}, u32[]{:S(2)}) collective-permute-start(bf16[864,128]{1,0:T(8,128)(2,1)} %bitcast.26), channel_id=1, source_target_pairs={{0,2},{1,3},{2,0},{3,1},{4,6},{5,7},{6,4},{7,5},{8,10},{9,11},{10,... | collective-permute-start | bytes 663560 | tf_op jit(solution)/shard_map/ppermute | solution.py:430
  13.2 59.5 %collective-permute-start.6 = (bf16[864,128]{1,0:T(8,128)(2,1)}, bf16[864,128]{1,0:T(8,128)(2,1)}, u32[]{:S(2)}, u32[]{:S(2)}) collective-permute-start(bf16[864,128]{1,0:T(8,128)(2,1)} %bitcast.26), channel_id=1, source_target_pairs={{0,3},{1,0},{2,1},{3,2},{4,7},{5,4},{6,5},{7,6},{8,11},{9,8},{10,9... | collective-permute-start | bytes 663560 | tf_op jit(solution)/shard_map/ppermute | solution.py:430
  19.2 1.0 copy-start.19
  24.2 1.6 %copy-start.13 = (f32[512,64]{0,1:T(8,128)S(1)}, f32[512,64]{0,1:T(8,128)}, u32[]{:S(2)}) copy-start(f32[512,64]{0,1:T(8,128)} %convolution_add_fusion.3) | copy-start | bytes 393220
  30.7 14.0 %collective-permute-start.2 = (bf16[1,1,8,8,128]{4,3,2,0,1:T(8,128)(2,1)S(1)}, bf16[1,1,8,8,128]{4,3,2,0,1:T(8,128)(2,1)}, u32[]{:S(2)}, u32[]{:S(2)}) collective-permute-start(bf16[1,1,8,8,128]{4,3,2,0,1:T(8,128)(2,1)S(1)} %fusion.8), channel_id=1, source_target_pairs={{0,4},{4,8},{8,12},{12,16},{16,20},{20,24},{24,28},{1,5},{5,9},{9,... | collective-permute-start | bytes 49160 | tf_op jit(solution)/shard_map/ppermute | solution.py:18
  35.2 9.5 %collective-permute-start.3 = (bf16[1,1,8,8,128]{4,3,2,0,1:T(8,128)(2,1)S(1)}, bf16[1,1,8,8,128]{4,3,2,0,1:T(8,128)(2,1)}, u32[]{:S(2)}, u32[]{:S(2)}) collective-permute-start(bf16[1,1,8,8,128]{4,3,2,0,1:T(8,128)(2,1)S(1)} %fusion.8), channel_id=1, source_target_pairs={{4,0},{8,4},{12,8},{16,12},{20,16},{24,20},{28,24},{5,1},{9,5},{13... | collective-permute-start | bytes 49160 | tf_op jit(solution)/shard_map/ppermute | solution.py:19
  38.1 4.7 %copy-start.8 = (bf16[1,3,3,64,64]{4,2,1,0,3:T(4,128)(2,1)S(1)}, bf16[1,3,3,64,64]{4,2,1,0,3:T(4,128)(2,1)}, u32[]{:S(2)}) copy-start(bf16[1,3,3,64,64]{4,2,1,0,3:T(4,128)(2,1)} %get-tuple-element.24) | copy-start | bytes 221188
  51.8 0.9 copy-start.7
  75.3 1.1 copy-start.1
  105.1 2.9 %copy-start.3 = (f32[4,8,48,128]{3,2,1,0:T(8,128)S(1)}, f32[4,8,48,128]{3,2,1,0:T(8,128)}, u32[]{:S(2)}) copy-start(f32[4,8,48,128]{3,2,1,0:T(8,128)} %get-tuple-element.7) | copy-start | bytes 2359300
  109.1 9.4 %collective-permute-start.7 = (bf16[1,1,16,16,64]{4,3,2,1,0:T(8,128)(2,1)}, bf16[1,1,16,16,64]{4,3,2,1,0:T(8,128)(2,1)S(1)}, u32[]{:S(2)}, u32[]{:S(2)}) collective-permute-start(bf16[1,1,16,16,64]{4,3,2,1,0:T(8,128)(2,1)} %get-tuple-element.90), channel_id=1, source_target_pairs={{0,4},{4,8},{8,12},{12,16},{16,20},{20,24},{24,28},{1,5},{5,9},{9,... | collective-permute-start | bytes 98312 | tf_op jit(solution)/shard_map/ppermute | solution.py:18
  112.5 5.9 %collective-permute-start.8 = (bf16[1,1,16,16,64]{4,3,2,1,0:T(8,128)(2,1)}, bf16[1,1,16,16,64]{4,3,2,1,0:T(8,128)(2,1)}, u32[]{:S(2)}, u32[]{:S(2)}) collective-permute-start(bf16[1,1,16,16,64]{4,3,2,1,0:T(8,128)(2,1)} %get-tuple-element.91), channel_id=1, source_target_pairs={{4,0},{8,4},{12,8},{16,12},{20,16},{24,20},{28,24},{5,1},{9,5},{13... | collective-permute-start | bytes 98312 | tf_op jit(solution)/shard_map/ppermute | solution.py:19
  114.7 1.1 copy-start.2
  121.4 11.6 %copy-start.4 = (f32[512,64]{0,1:T(8,128)S(1)}, f32[512,64]{0,1:T(8,128)}, u32[]{:S(2)}) copy-start(f32[512,64]{0,1:T(8,128)} %convolution_add_fusion.2) | copy-start | bytes 393220
  127.1 6.9 %copy-start.12 = (bf16[1,3,3,64,64]{4,3,2,1,0:T(8,128)(2,1)S(1)}, bf16[1,3,3,64,64]{4,3,2,1,0:T(8,128)(2,1)}, u32[]{:S(2)}) copy-start(bf16[1,3,3,64,64]{4,3,2,1,0:T(8,128)(2,1)} %copy.55) | copy-start | bytes 221188
  130.4 3.5 %copy-start.17 = (bf16[512,64]{0,1:T(8,128)(2,1)S(1)}, bf16[512,64]{0,1:T(8,128)(2,1)}, u32[]{:S(2)}) copy-start(bf16[512,64]{0,1:T(8,128)(2,1)} %copy.52) | copy-start | bytes 196612
  130.5 3.5 %copy-start.16 = (bf16[512,64]{0,1:T(8,128)(2,1)S(1)}, bf16[512,64]{0,1:T(8,128)(2,1)}, u32[]{:S(2)}) copy-start(bf16[512,64]{0,1:T(8,128)(2,1)} %copy.53) | copy-start | bytes 196612
  133.0 1.3 copy-start.21
  (7 other events, 5.8 us)
